TPU v7x, 32 devices: a whole 2x2x4 slice. The times are simulated.
32 devices in a mesh: survey: 4 (over z), tile: 8 (over y, x, core).
Axes of the slice: x: 2, y: 2, z: 4, core: 2. Of those that a mesh axis runs over, the one named last changes fastest.
Arguments:
- data: bfloat16 [4, 64, 128, 256], P('survey', 'tile'), may hold values from -12 to 12
- correlation_index: int32 [4, 8, 4, 128], P(None, 'tile'), may hold values from 0 to 1023, as said below
- correlation_count: int32 [4, 8, 4], P(None, 'tile'), may hold values from 0 to 128, as said below
- smoothing: float32 [3], replicated, may hold values from 0.5 to 4
Outputs:
- fields: float32 [4, 3, 64, 128], P('survey', None, 'tile')
- volume: bfloat16 [4, 64, 128, 256], P('survey', 'tile')
Inputs may be any that keep to these rules, and one draw needn't show every extreme that they name: `correlation_index`: each list holds 128 consecutive positions of the tile. `correlation_count`: zero where s equals p; one or more where s is p + 1 modulo 4; in every draw one tile and one destination group receive 128 live slots from every other group.
All inputs are finite; a program needn't handle non-finite values.
Results may differ from a plain program's by a relative error of at most 0.0014.
Values may be sent and summed in bfloat16 or wider, within the bound.
No kernel may reach another device: no remote copies, remote signals or barrier semaphores. Data moves between devices by JAX's collectives and lax.ppermute only.
A program may use at most 64 MiB of HBM per device.

v0:
```python
import functools

import jax
import jax.numpy as jnp
from jax import lax
from jax.experimental import pallas as pl
from jax.experimental.pallas import tpu as pltpu
from jax.sharding import PartitionSpec as P


CG_ITERS = 3

damping = 0.05
sim_eps = 1e-05

f32 = jnp.float32
bf16 = jnp.bfloat16
VMEM = pl.BlockSpec(memory_space=pltpu.VMEM)
ANY = pl.BlockSpec(memory_space=pl.ANY)
PARAMS = pltpu.CompilerParams(vmem_limit_bytes=16 * 1024 * 1024)
NT = (((1,), (1,)), ((), ()))


def is_power(n):
    return n & (n - 1) == 0


def receiver(me, k, n):
    return me ^ k if is_power(n) else lax.rem(me + k, n)


def sender(me, k, n):
    return me ^ k if is_power(n) else lax.rem(me + n - k, n)


def survey_pairs(k, n):
    return [(i, i ^ k if is_power(n) else (i + k) % n) for i in range(n)]


def iota(shape, dim):
    return lax.broadcasted_iota(jnp.int32, shape, dim)


def time_of(sample, samples):
    return (sample.astype(f32) - (samples - 1) / 2.0) / (samples / 2.0)


def time_column(samples, lanes):
    return time_of(iota((samples, lanes), 0), samples)


def joined_blocks(data_ref, start, rows_x, rows_y):
    block = start // rows_y
    split = start - block * rows_y
    after = jnp.minimum(block + 1, rows_x - 1)
    here = data_ref[pl.ds(pl.multiple_of(block * rows_y, rows_y), rows_y), :].astype(f32)
    there = data_ref[pl.ds(pl.multiple_of(after * rows_y, rows_y), rows_y), :].astype(f32)
    return jnp.where(iota(here.shape, 0) >= split, here, there).astype(data_ref.dtype)


def pack_kernel(n, rows_x, index_ref, data_ref, *out_refs):
    me = lax.axis_index("survey")
    rows_y = data_ref.shape[0] // rows_x
    for k in range(1, n):
        start = jnp.min(index_ref[me, pl.ds(receiver(me, k, n), 1), :])
        out_refs[k - 1][...] = joined_blocks(data_ref, start, rows_x, rows_y)


def put_rows(ref, k, rows):
    for i, row in enumerate(rows):
        ref[k, i : i + 1, :] = row


def mean_over(values):
    return jnp.sum(values, axis=0, keepdims=True) * (1.0 / values.shape[0])


def energy_rows(vals, moved, time_pos):
    tilted = time_pos * vals
    return [mean_over(moved * moved), mean_over(vals * vals), mean_over(tilted * tilted)]


def prepare_kernel(n, index_ref, count_ref, data_ref, basis_ref, own_ref, moved_ref, mask_ref, energy_ref, slope_ref):
    me = lax.axis_index("survey")
    samples, rows_y = own_ref.shape[1:]
    rows_x = data_ref.shape[0] // rows_y
    row, col = iota((samples, samples), 0), iota((samples, samples), 1)
    basis_ref[:samples, :] = jnp.where(row == col, 1.0, 0.0).astype(bf16)
    basis_ref[samples:, :] = (jnp.where(col == row + 1, 0.5, 0.0) - jnp.where(col == row - 1, 0.5, 0.0)).astype(bf16)
    time_pos = time_column(samples, rows_y)
    position = iota((rows_x, rows_y), 0) * rows_y + iota((rows_x, rows_y), 1)
    for k in range(1, n):
        source = sender(me, k, n)
        start = jnp.min(index_ref[source, pl.ds(me, 1), :])
        counts = count_ref[source]
        count = jnp.sum(jnp.where(iota(counts.shape, 1) == me, counts, 0))
        mask_ref[k - 1] = jnp.where((position >= start) & (position < start + count), 1.0, 0.0)
        rows = joined_blocks(data_ref, start, rows_x, rows_y)
        both = lax.dot_general(basis_ref[...], rows, NT, preferred_element_type=f32)
        own_ref[k - 1] = both[:samples]
        moved_ref[k - 1] = both[samples:]
        put_rows(energy_ref, k - 1, energy_rows(both[:samples], both[samples:], time_pos))
    for x in range(rows_x):
        block = slice(x * rows_y, (x + 1) * rows_y)
        slope_ref[block, :] = lax.dot_general(data_ref[block, :], basis_ref[samples:, :], NT, preferred_element_type=f32)


def corrected_lanes(values, moved, fields_ref, mask, time_pos):
    shift, gain, trend = [jnp.sum(fields_ref[c] * mask, axis=0, keepdims=True) for c in range(3)]
    amplitude = jnp.exp(gain + trend * time_pos)
    return (amplitude * (values + shift * moved)).astype(bf16)


def refresh_kernel(n, fields_ref, basis_ref, own_ref, moved_ref, mask_ref, *refs):
    arrived = refs[: n - 1]
    new_own_ref, new_moved_ref, energy_ref, partner_ref, partner_moved_ref = refs[n - 1 :]
    samples, rows_y = own_ref.shape[1:]
    time_pos = time_column(samples, rows_y)
    for k in range(n - 1):
        rounded = corrected_lanes(own_ref[k], moved_ref[k], fields_ref, mask_ref[k], time_pos)
        vals = rounded.astype(f32)
        moved = jnp.dot(basis_ref[samples:, :], rounded, preferred_element_type=f32)
        new_own_ref[k] = vals
        new_moved_ref[k] = moved
        put_rows(energy_ref, k, energy_rows(vals, moved, time_pos))
        both = lax.dot_general(basis_ref[...], arrived[k][...], NT, preferred_element_type=f32)
        partner_ref[k] = both[:samples]
        partner_moved_ref[k] = both[samples:]


def add_pair(sums, own, moved, partner, mask, energy_ref, k, time_pos):
    residual = partner - own
    along = residual * own
    slope_sum = mean_over(residual * moved)
    gain_sum = mean_over(along)
    trend_sum = mean_over(time_pos * along)
    cross_term = mean_over(own * partner)
    other_energy = mean_over(partner * partner)
    energy = [energy_ref[k, i : i + 1, :] for i in range(3)]
    weight = cross_term * cross_term / ((energy[1] + sim_eps) * (other_energy + sim_eps))
    for c, row in enumerate([slope_sum, gain_sum, trend_sum] + energy):
        term = mask * (weight * row)
        sums[c] = term if sums[c] is None else sums[c] + term


def pair_first_kernel(n, basis_ref, own_ref, moved_ref, mask_ref, energy_ref, *refs):
    arrived, out_ref = refs[: n - 1], refs[-1]
    samples, rows_y = own_ref.shape[1:]
    time_pos = time_column(samples, rows_y)
    sums = [None] * 6
    for k in range(n - 1):
        partner = lax.dot_general(basis_ref[:samples, :], arrived[k][...], NT, preferred_element_type=f32)
        add_pair(sums, own_ref[k], moved_ref[k], partner, mask_ref[k], energy_ref, k, time_pos)
    for c in range(6):
        out_ref[c] = sums[c]


def pair_next_kernel(n, own_ref, moved_ref, mask_ref, energy_ref, partner_ref, partner_moved_ref, *refs):
    field_refs, out_ref = refs[: n - 1], refs[-1]
    samples, rows_y = own_ref.shape[1:]
    time_pos = time_column(samples, rows_y)
    sums = [None] * 6
    for k in range(n - 1):
        partner = corrected_lanes(partner_ref[k], partner_moved_ref[k], field_refs[k], mask_ref[k], time_pos)
        add_pair(sums, own_ref[k], moved_ref[k], partner.astype(f32), mask_ref[k], energy_ref, k, time_pos)
    for c in range(6):
        out_ref[c] = sums[c]


def grid_solve(masks, smoothing_ref, piece_refs, grid_ref, tile):
    rows_x = piece_refs[0].shape[1]
    for piece, mask in zip(piece_refs, masks):
        spot = pl.multiple_of((tile ^ mask) * rows_x, rows_x)
        for c in range(6):
            grid_ref[c, pl.ds(spot, rows_x), :] = piece[c]
    size_x, size_y = grid_ref.shape[1:]
    grid_x = iota((size_x, size_y), 0)
    grid_y = iota((size_x, size_y), 1)
    each = range(3)

    def total(q):
        return jnp.sum(jnp.sum(q, axis=0, keepdims=True), axis=1, keepdims=True)

    def beside(v):
        return (
            jnp.where(grid_x > 0, pltpu.roll(v, 1, 0), 0.0)
            + jnp.where(grid_x < size_x - 1, pltpu.roll(v, size_x - 1, 0), 0.0)
            + jnp.where(grid_y > 0, pltpu.roll(v, 1, 1), 0.0)
            + jnp.where(grid_y < size_y - 1, pltpu.roll(v, size_y - 1, 1), 0.0)
        )

    strength = [smoothing_ref[0:1, c : c + 1] for c in each]
    diagonal = [grid_ref[3 + c] + (damping + 4.0 * strength[c]) for c in each]

    def apply(v):
        near = [beside(v[c]) for c in each]
        return [diagonal[c] * v[c] - strength[c] * near[c] for c in each]

    residual = [grid_ref[c] for c in each]
    image = apply(residual)
    norm_now = [total(residual[c] * residual[c]) for c in each]
    product = [total(residual[c] * image[c]) for c in each]
    alpha = [norm_now[c] / product[c] for c in each]
    direction, along = residual, image
    update = [alpha[c] * direction[c] for c in each]
    for iteration in range(1, CG_ITERS):
        residual = [residual[c] - alpha[c] * along[c] for c in each]
        image = apply(residual)
        norm_next = [total(residual[c] * residual[c]) for c in each]
        product = [total(residual[c] * image[c]) for c in each]
        ratio = [norm_next[c] / norm_now[c] for c in each]
        alpha = [norm_next[c] / (product[c] - ratio[c] * norm_next[c] / alpha[c]) for c in each]
        direction = [residual[c] + ratio[c] * direction[c] for c in each]
        if iteration + 1 < CG_ITERS:
            along = [image[c] + ratio[c] * along[c] for c in each]
        update = [update[c] + alpha[c] * direction[c] for c in each]
        norm_now = norm_next
    return update


def tile_part(grid_ref, c, tile, rows_x):
    return grid_ref[c, pl.ds(pl.multiple_of(tile * rows_x, rows_x), rows_x), :]


def solve_first_kernel(masks, smoothing_ref, *refs):
    pieces = refs[: len(masks)]
    fields_ref, beside_ref, grid_ref = refs[len(masks) :]
    tile = lax.axis_index("tile")
    updates = grid_solve(masks, smoothing_ref, pieces, grid_ref, tile)
    for c in range(3):
        grid_ref[c] = updates[c]
        fields_ref[c] = tile_part(grid_ref, c, tile, fields_ref.shape[1])
        beside_ref[c] = tile_part(grid_ref, c, tile ^ 1, fields_ref.shape[1])


def three_parts(values):
    parts = []
    for _ in range(3):
        part = values.astype(bf16).astype(f32)
        parts.append(part)
        values = values - part
    return parts


def solve_last_kernel(masks, smoothing_ref, before_ref, data_ref, slope_ref, *refs):
    pieces = refs[: len(masks)]
    fields_ref, volume_ref, grid_ref, block_ref, sems = refs[len(masks) :]
    tile = lax.axis_index("tile")
    rows_x, rows_y = fields_ref.shape[1:]
    samples = data_ref.shape[1]
    lanes = 16 * rows_x
    kind = iota((lanes, samples), 0) // rows_x
    time_pos = time_of(iota((lanes, samples), 1), samples)
    spread_power = jnp.where((kind >= 3) & (kind < 6), 1.0, jnp.where((kind >= 6) & (kind < 9), time_pos, 0.0))
    spread_shift = jnp.where(kind < 3, 1.0, 0.0)
    spread = jnp.concatenate([spread_shift, spread_power], axis=1).astype(bf16)
    which = lax.rem(iota((rows_y, lanes), 1), rows_x)
    updates = grid_solve(masks, smoothing_ref, pieces, grid_ref, tile)
    parts = []
    for c in range(3):
        grid_ref[c] = updates[c]
        mine = before_ref[c] + tile_part(grid_ref, c, tile, rows_x)
        fields_ref[c] = mine
        parts += three_parts(mine)
    parts.append(jnp.zeros((lanes - 9 * rows_x, rows_y), f32))
    columns = jnp.transpose(jnp.concatenate(parts, axis=0))
    copies = []
    for x in range(rows_x):
        rows = slice(x * rows_y, (x + 1) * rows_y)
        mine = jnp.where(which == x, columns, 0.0).astype(bf16)
        both = jnp.dot(mine, spread, preferred_element_type=f32)
        shift, power = both[:, :samples], both[:, samples:]
        moved = data_ref[rows, :].astype(f32) + shift * slope_ref[rows, :]
        block_ref[rows, :] = (jnp.exp(power) * moved).astype(volume_ref.dtype)
        copy = pltpu.make_async_copy(block_ref.at[rows, :], volume_ref.at[rows, :], sems.at[x])
        copy.start()
        copies.append(copy)
    for copy in copies:
        copy.wait()


def gather_tiles(piece, n):
    pieces = {0: piece}
    for mask in range(3, n, 2):
        pieces[mask] = lax.ppermute(piece, "tile", [(i, i ^ mask) for i in range(n)])
    if n > 1:
        for mask in list(pieces):
            pieces[mask ^ 1] = lax.ppermute(pieces[mask], "tile", [(i, i ^ 1) for i in range(n)])
    masks = sorted(pieces)
    return masks, [pieces[m] for m in masks]


def exchange(arrays, n):
    got = []
    for k in range(1, n):
        got.append(lax.ppermute(arrays[k - 1], "survey", survey_pairs(k, n)))
    return got


def exchange_across(array, n, n_tile):
    got = []
    for k in range(1, n):
        pairs = [(s * n_tile + t, d * n_tile + (t ^ 1)) for s, d in survey_pairs(k, n) for t in range(n_tile)]
        got.append(lax.ppermute(array, ("survey", "tile"), pairs))
    return got


def call(kernel, out_shape, n_in, **options):
    single = not isinstance(out_shape, list)
    options = {"out_specs": VMEM if single else [VMEM] * len(out_shape), **options}
    return pl.pallas_call(kernel, out_shape=out_shape, in_specs=[VMEM] * n_in, compiler_params=PARAMS, **options)


def local(n_survey, n_tile, data, correlation_index, correlation_count, smoothing):
    rows_x, rows_y, samples = data.shape[1:]
    total, cap = rows_x * rows_y, correlation_index.shape[-1]
    assert cap <= rows_y and samples <= 256 and is_power(samples) and is_power(n_tile) and n_tile > 1
    others = n_survey - 1
    raw = data.reshape(total, samples)
    index = correlation_index[:, 0]
    smoothing = smoothing.reshape(1, 3)
    packed = jax.ShapeDtypeStruct((rows_y, samples), data.dtype)
    field_shape = jax.ShapeDtypeStruct((3, rows_x, rows_y), f32)
    term_shape = jax.ShapeDtypeStruct((6, rows_x, rows_y), f32)
    lane_shape = jax.ShapeDtypeStruct((others, samples, rows_y), f32)
    mask_shape = jax.ShapeDtypeStruct((others, rows_x, rows_y), f32)
    energy_shape = jax.ShapeDtypeStruct((others, 8, rows_y), f32)
    basis_shape = jax.ShapeDtypeStruct((2 * samples, samples), bf16)
    slope_shape = jax.ShapeDtypeStruct((total, samples), f32)
    volume_shape = jax.ShapeDtypeStruct((total, samples), data.dtype)
    grid = pltpu.VMEM((6, rows_x * n_tile, rows_y), f32)

    outgoing = call(functools.partial(pack_kernel, n_survey, rows_x), [packed] * others, 2)(index, raw)
    arrived = exchange(outgoing, n_survey)
    basis, own, moved, mask, energy, slope = call(
        functools.partial(prepare_kernel, n_survey),
        [basis_shape, lane_shape, lane_shape, mask_shape, energy_shape, slope_shape],
        3,
    )(index, correlation_count, raw)
    terms = call(functools.partial(pair_first_kernel, n_survey), term_shape, 5 + others)(
        basis, own, moved, mask, energy, *arrived
    )
    masks, pieces = gather_tiles(terms, n_tile)
    fields, beside = call(
        functools.partial(solve_first_kernel, masks), [field_shape] * 2, 1 + n_tile, scratch_shapes=[grid]
    )(smoothing, *pieces)

    partner_fields = exchange_across(beside, n_survey, n_tile)
    own, moved, energy, partner, partner_moved = call(
        functools.partial(refresh_kernel, n_survey),
        [lane_shape, lane_shape, energy_shape, lane_shape, lane_shape],
        5 + others,
    )(fields, basis, own, moved, mask, *arrived)
    terms = call(functools.partial(pair_next_kernel, n_survey), term_shape, 6 + others)(
        own, moved, mask, energy, partner, partner_moved, *partner_fields
    )
    masks, pieces = gather_tiles(terms, n_tile)
    fields, volume = call(
        functools.partial(solve_last_kernel, masks),
        [field_shape, volume_shape],
        4 + n_tile,
        out_specs=[VMEM, ANY],
        scratch_shapes=[grid, pltpu.VMEM((total, samples), data.dtype), pltpu.SemaphoreType.DMA((rows_x,))],
    )(smoothing, fields, raw, slope, *pieces)
    return fields.reshape(1, 3, rows_x, rows_y), volume.reshape(1, rows_x, rows_y, samples)


def solution(mesh):
    placed = (
        P("survey", "tile", None, None),
        P(None, "tile", None, None),
        P(None, "tile", None),
        P(),
    )
    return jax.shard_map(
        functools.partial(local, mesh.shape["survey"], mesh.shape["tile"]),
        mesh=mesh,
        in_specs=placed,
        out_specs=(P("survey", None, "tile", None), P("survey", "tile", None, None)),
        check_vma=False,
    )
```

profile of v0, /device:TPU:0, one launch (start us, length us, event | category | flops | bytes accessed | tf_op | source)
XLA Modules:
  0.0 39.7 jit_solution(12749875198821197059)
XLA Ops:
  0.6 1.0 %copy-done = bf16[1,8,128,256]{3,2,1,0:T(8,128)(2,1)S(1)} copy-done((bf16[1,8,128,256]{3,2,1,0:T(8,128)(2,1)S(1)}, bf16[1,8,128,256]{3,2,1,0:T(8,128)(2,1)}, u32[]{:S(2)}) %copy-start) | copy-done | bytes 524312
  1.7 0.7 %copy-done.2 = s32[4,1,4,128]{3,2,1,0:T(4,128)S(1)} copy-done((s32[4,1,4,128]{3,2,1,0:T(4,128)S(1)}, s32[4,1,4,128]{3,2,1,0:T(4,128)}, u32[]{:S(2)}) %copy-start.2) | copy-done | bytes 8216
  2.7 3.1 %collective-permute-start = (bf16[128,256]{1,0:T(8,128)(2,1)S(1)}, bf16[128,256]{1,0:T(8,128)(2,1)S(1)}, u32[]{:S(2)}, u32[]{:S(2)}) collective-permute-start(bf16[128,256]{1,0:T(8,128)(2,1)S(1)} %get-tuple-element.25), channel_id=1, source_target_pairs={{0,8},{8,0},{16,24},{24,16},{1,9},{9,1},{17,25},{25,17},{2,10},{10... | collective-permute-start | bytes 196616 | tf_op jit(solution)/shard_map/ppermute | solution.py:296
  5.8 2.6 %collective-permute-start.1 = (bf16[128,256]{1,0:T(8,128)(2,1)S(1)}, bf16[128,256]{1,0:T(8,128)(2,1)S(1)}, u32[]{:S(2)}, u32[]{:S(2)}) collective-permute-start(bf16[128,256]{1,0:T(8,128)(2,1)S(1)} %get-tuple-element.26), channel_id=1, source_target_pairs={{0,16},{8,24},{16,0},{24,8},{1,17},{9,25},{17,1},{25,9},{2,18},{10... | collective-permute-start | bytes 196616 | tf_op jit(solution)/shard_map/ppermute | solution.py:296
  8.4 0.9 %shard_map.59 = (bf16[512,256]{1,0:T(8,128)(2,1)S(1)}, f32[3,256,128]{2,1,0:T(8,128)S(1)}, f32[3,256,128]{2,1,0:T(8,128)S(1)}, f32[3,8,128]{2,1,0:T(8,128)S(1)},...) custom-call(s32[4,4,128]{2,1,0:T(4,128)S(1)} %bitcast.9, s32[4,1,4]{2,1,0:T(1,128)S(1)} %copy-done.3, ...), custom_call_target="tpu_custom_call" | custom-call | tf_op jit(solution)/shard_map/pallas_call | solution.py:335
  9.3 3.8 %collective-permute-done.1.refs_1_ = bf16[128,256]{1,0:T(8,128)(2,1)S(1)} collective-permute-done((bf16[128,256]{1,0:T(8,128)(2,1)S(1)}, bf16[128,256]{1,0:T(8,128)(2,1)S(1)}, u32[]{:S(2)}, u32[]{:S(2)}) %collective-permute-start.1) | collective-permute-done | bytes 65568 | tf_op jit(solution)/shard_map/ppermute | solution.py:296
  13.0 1.4 %collective-permute-done.2.refs_2_ = bf16[128,256]{1,0:T(8,128)(2,1)S(1)} collective-permute-done((bf16[128,256]{1,0:T(8,128)(2,1)S(1)}, bf16[128,256]{1,0:T(8,128)(2,1)S(1)}, u32[]{:S(2)}, u32[]{:S(2)}) %collective-permute-start.2) | collective-permute-done | bytes 65568 | tf_op jit(solution)/shard_map/ppermute | solution.py:296
  14.9 2.7 %collective-permute-start.6 = (f32[6,8,128]{2,1,0:T(8,128)S(1)}, f32[6,8,128]{2,1,0:T(8,128)S(1)}, u32[]{:S(2)}, u32[]{:S(2)}) collective-permute-start(f32[6,8,128]{2,1,0:T(8,128)S(1)} %shard_map.61.refs_0_), channel_id=1, source_target_pairs={{0,5},{1,4},{2,7},{3,6},{4,1},{5,0},{6,3},{7,2},{8,13},{9,12},{10,... | collective-permute-start | bytes 73736 | tf_op jit(solution)/shard_map/ppermute | solution.py:285
  17.6 0.6 %collective-permute-start.3 = (f32[6,8,128]{2,1,0:T(8,128)S(1)}, f32[6,8,128]{2,1,0:T(8,128)S(1)}, u32[]{:S(2)}, u32[]{:S(2)}) collective-permute-start(f32[6,8,128]{2,1,0:T(8,128)S(1)} %shard_map.61.refs_0_), channel_id=1, source_target_pairs={{0,1},{1,0},{2,3},{3,2},{4,5},{5,4},{6,7},{7,6},{8,9},{9,8},{10,11... | collective-permute-start | bytes 73736 | tf_op jit(solution)/shard_map/ppermute | solution.py:288
  18.4 0.7 %collective-permute-done.6.refs_5_ = f32[6,8,128]{2,1,0:T(8,128)S(1)} collective-permute-done((f32[6,8,128]{2,1,0:T(8,128)S(1)}, f32[6,8,128]{2,1,0:T(8,128)S(1)}, u32[]{:S(2)}, u32[]{:S(2)}) %collective-permute-start.6) | collective-permute-done | bytes 24608 | tf_op jit(solution)/shard_map/ppermute | solution.py:285
  19.1 0.6 %collective-permute-start.7 = (f32[6,8,128]{2,1,0:T(8,128)S(1)}, f32[6,8,128]{2,1,0:T(8,128)S(1)}, u32[]{:S(2)}, u32[]{:S(2)}) collective-permute-start(f32[6,8,128]{2,1,0:T(8,128)S(1)} %collective-permute-done.6.refs_5_), channel_id=1, source_target_pairs={{0,1},{1,0},{2,3},{3,2},{4,5},{5,4},{6,7},{7,6},{8,9},{9,8},{10,11... | collective-permute-start | bytes 73736 | tf_op jit(solution)/shard_map/ppermute | solution.py:288
  19.7 2.0 %collective-permute-done.8.refs_7_ = f32[6,8,128]{2,1,0:T(8,128)S(1)} collective-permute-done((f32[6,8,128]{2,1,0:T(8,128)S(1)}, f32[6,8,128]{2,1,0:T(8,128)S(1)}, u32[]{:S(2)}, u32[]{:S(2)}) %collective-permute-start.8) | collective-permute-done | bytes 24608 | tf_op jit(solution)/shard_map/ppermute | solution.py:285
  21.8 1.2 %collective-permute-done.9.refs_6_ = f32[6,8,128]{2,1,0:T(8,128)S(1)} collective-permute-done((f32[6,8,128]{2,1,0:T(8,128)S(1)}, f32[6,8,128]{2,1,0:T(8,128)S(1)}, u32[]{:S(2)}, u32[]{:S(2)}) %collective-permute-start.9) | collective-permute-done | bytes 24608 | tf_op jit(solution)/shard_map/ppermute | solution.py:288
  22.9 0.6 %shard_map.62 = (f32[3,8,128]{2,1,0:T(8,128)S(1)}, f32[3,8,128]{2,1,0:T(8,128)S(1)}) custom-call(f32[1,3]{1,0:T(1,128)S(1)} %bitcast.10, f32[6,8,128]{2,1,0:T(8,128)S(1)} %shard_map.61.refs_0_, f32[6,8,128]{2,1,0:T(8,128)S(1)} %collective-permute-done.3.refs_1_, f32[6,8,128]{2,1,0:T(8,128)S(1)} %collective-permute-done.5.refs_2_, ...), custom_call_target="tpu_custom_call" | custom-call | tf_op jit(solution)/shard_map/pallas_call | solution.py:344
  23.7 2.0 %collective-permute-start.11 = (f32[3,8,128]{2,1,0:T(8,128)S(1)}, f32[3,8,128]{2,1,0:T(8,128)S(1)}, u32[]{:S(2)}, u32[]{:S(2)}) collective-permute-start(f32[3,8,128]{2,1,0:T(8,128)S(1)} %get-tuple-element.35), channel_id=1, source_target_pairs={{0,17},{1,16},{2,19},{3,18},{4,21},{5,20},{6,23},{7,22},{8,25},{9,... | collective-permute-start | bytes 36872 | tf_op jit(solution)/shard_map/ppermute | solution.py:304
  25.7 1.8 %collective-permute-start.12 = (f32[3,8,128]{2,1,0:T(8,128)S(1)}, f32[3,8,128]{2,1,0:T(8,128)S(1)}, u32[]{:S(2)}, u32[]{:S(2)}) collective-permute-start(f32[3,8,128]{2,1,0:T(8,128)S(1)} %get-tuple-element.35), channel_id=1, source_target_pairs={{0,25},{1,24},{2,27},{3,26},{4,29},{5,28},{6,31},{7,30},{8,17},{9,... | collective-permute-start | bytes 36872 | tf_op jit(solution)/shard_map/ppermute | solution.py:304
  27.5 0.5 %shard_map.63 = (f32[3,256,128]{2,1,0:T(8,128)S(1)}, f32[3,256,128]{2,1,0:T(8,128)S(1)}, f32[3,8,128]{2,1,0:T(8,128)S(1)}, f32[3,256,128]{2,1,0:T(8,128)S(1)}, f32[3,256,128]{2,1,0:T(8,128)S(1)}) custom-call(f32[3,8,128]{2,1,0:T(8,128)S(1)} %get-tuple-element.28.fields_ref.before_ref, bf16[512,256]{1,0:T(8,128)(2,1)S(1)} %get-tuple-element.20.basis_ref, ...), custom_call_target="tpu_custom_call" | custom-call | tf_op jit(solution)/shard_map/pallas_call | solution.py:349
  28.1 2.5 %collective-permute-done.12.refs_2_ = f32[3,8,128]{2,1,0:T(8,128)S(1)} collective-permute-done((f32[3,8,128]{2,1,0:T(8,128)S(1)}, f32[3,8,128]{2,1,0:T(8,128)S(1)}, u32[]{:S(2)}, u32[]{:S(2)}) %collective-permute-start.12) | collective-permute-done | bytes 12320 | tf_op jit(solution)/shard_map/ppermute | solution.py:304
  31.0 0.5 %collective-permute-start.14 = (f32[6,8,128]{2,1,0:T(8,128)S(1)}, f32[6,8,128]{2,1,0:T(8,128)S(1)}, u32[]{:S(2)}, u32[]{:S(2)}) collective-permute-start(f32[6,8,128]{2,1,0:T(8,128)S(1)} %shard_map.64.refs_0_), channel_id=1, source_target_pairs={{0,3},{1,2},{2,1},{3,0},{4,7},{5,6},{6,5},{7,4},{8,11},{9,10},{10,... | collective-permute-start | bytes 73736 | tf_op jit(solution)/shard_map/ppermute | solution.py:285
  31.5 0.5 %collective-permute-start.16 = (f32[6,8,128]{2,1,0:T(8,128)S(1)}, f32[6,8,128]{2,1,0:T(8,128)S(1)}, u32[]{:S(2)}, u32[]{:S(2)}) collective-permute-start(f32[6,8,128]{2,1,0:T(8,128)S(1)} %shard_map.64.refs_0_), channel_id=1, source_target_pairs={{0,5},{1,4},{2,7},{3,6},{4,1},{5,0},{6,3},{7,2},{8,13},{9,12},{10,... | collective-permute-start | bytes 73736 | tf_op jit(solution)/shard_map/ppermute | solution.py:285
  32.0 2.1 %collective-permute-start.18 = (f32[6,8,128]{2,1,0:T(8,128)S(1)}, f32[6,8,128]{2,1,0:T(8,128)S(1)}, u32[]{:S(2)}, u32[]{:S(2)}) collective-permute-start(f32[6,8,128]{2,1,0:T(8,128)S(1)} %shard_map.64.refs_0_), channel_id=1, source_target_pairs={{0,7},{1,6},{2,5},{3,4},{4,3},{5,2},{6,1},{7,0},{8,15},{9,14},{10,... | collective-permute-start | bytes 73736 | tf_op jit(solution)/shard_map/ppermute | solution.py:285
  35.1 1.0 %collective-permute-done.18.refs_7_ = f32[6,8,128]{2,1,0:T(8,128)S(1)} collective-permute-done((f32[6,8,128]{2,1,0:T(8,128)S(1)}, f32[6,8,128]{2,1,0:T(8,128)S(1)}, u32[]{:S(2)}, u32[]{:S(2)}) %collective-permute-start.18) | collective-permute-done | bytes 24608 | tf_op jit(solution)/shard_map/ppermute | solution.py:285
  36.3 1.0 %collective-permute-done.19.refs_6_ = f32[6,8,128]{2,1,0:T(8,128)S(1)} collective-permute-done((f32[6,8,128]{2,1,0:T(8,128)S(1)}, f32[6,8,128]{2,1,0:T(8,128)S(1)}, u32[]{:S(2)}, u32[]{:S(2)}) %collective-permute-start.19) | collective-permute-done | bytes 24608 | tf_op jit(solution)/shard_map/ppermute | solution.py:288
  37.3 2.4 %shard_map.65 = (f32[3,8,128]{2,1,0:T(8,128)}, bf16[1024,256]{1,0:T(8,128)(2,1)}) custom-call(f32[1,3]{1,0:T(1,128)S(1)} %bitcast.11, f32[3,8,128]{2,1,0:T(8,128)S(1)} %get-tuple-element.28.fields_ref.before_ref, bf16[1024,256]{1,0:T(8,128)(2,1)S(1)} %bitcast.7, f32[1024,256]{1,0:T(8,128)S(1)} %get-tuple-element.29.slope_ref, ...), custom_call_target="tpu_custom_call" | custom-call | tf_op jit(solution)/shard_map/pallas_call | solution.py:358
  (33 shorter events, 2.7 us)
Async XLA Ops:
  0.6 1.0 %copy-start = (bf16[1,8,128,256]{3,2,1,0:T(8,128)(2,1)S(1)}, bf16[1,8,128,256]{3,2,1,0:T(8,128)(2,1)}, u32[]{:S(2)}) copy-start(bf16[1,8,128,256]{3,2,1,0:T(8,128)(2,1)} %param.4) | copy-start | bytes 1572868
  2.4 6.0 %copy-start.1 = (bf16[1,8,128,256]{3,2,1,0:T(8,128)(2,1)S(1)}, bf16[1,8,128,256]{3,2,1,0:T(8,128)(2,1)}, u32[]{:S(2)}) copy-start(bf16[1,8,128,256]{3,2,1,0:T(8,128)(2,1)} %param.4) | copy-start | bytes 1572868
  2.6 5.7 %copy-start.3 = (s32[4,1,4]{2,1,0:T(1,128)S(1)}, s32[4,1,4]{2,1,0:T(1,128)}, u32[]{:S(2)}) copy-start(s32[4,1,4]{2,1,0:T(1,128)} %count_ref.1) | copy-start | bytes 196
  2.7 6.6 %collective-permute-start = (bf16[128,256]{1,0:T(8,128)(2,1)S(1)}, bf16[128,256]{1,0:T(8,128)(2,1)S(1)}, u32[]{:S(2)}, u32[]{:S(2)}) collective-permute-start(bf16[128,256]{1,0:T(8,128)(2,1)S(1)} %get-tuple-element.25), channel_id=1, source_target_pairs={{0,8},{8,0},{16,24},{24,16},{1,9},{9,1},{17,25},{25,17},{2,10},{10... | collective-permute-start | bytes 196616 | tf_op jit(solution)/shard_map/ppermute | solution.py:296
  5.8 7.3 %collective-permute-start.1 = (bf16[128,256]{1,0:T(8,128)(2,1)S(1)}, bf16[128,256]{1,0:T(8,128)(2,1)S(1)}, u32[]{:S(2)}, u32[]{:S(2)}) collective-permute-start(bf16[128,256]{1,0:T(8,128)(2,1)S(1)} %get-tuple-element.26), channel_id=1, source_target_pairs={{0,16},{8,24},{16,0},{24,8},{1,17},{9,25},{17,1},{25,9},{2,18},{10... | collective-permute-start | bytes 196616 | tf_op jit(solution)/shard_map/ppermute | solution.py:296
  8.4 6.1 %collective-permute-start.2 = (bf16[128,256]{1,0:T(8,128)(2,1)S(1)}, bf16[128,256]{1,0:T(8,128)(2,1)S(1)}, u32[]{:S(2)}, u32[]{:S(2)}) collective-permute-start(bf16[128,256]{1,0:T(8,128)(2,1)S(1)} %get-tuple-element.27), channel_id=1, source_target_pairs={{0,24},{8,16},{16,8},{24,0},{1,25},{9,17},{17,9},{25,1},{2,26},{10... | collective-permute-start | bytes 196616 | tf_op jit(solution)/shard_map/ppermute | solution.py:296
  14.8 8.2 %copy-start.4 = (f32[3]{0:T(128)S(1)}, f32[3]{0:T(128)}, u32[]{:S(2)}) copy-start(f32[3]{0:T(128)} %param.7) | copy-start | bytes 40
  14.8 3.5 %collective-permute-start.4 = (f32[6,8,128]{2,1,0:T(8,128)S(1)}, f32[6,8,128]{2,1,0:T(8,128)S(1)}, u32[]{:S(2)}, u32[]{:S(2)}) collective-permute-start(f32[6,8,128]{2,1,0:T(8,128)S(1)} %shard_map.61.refs_0_), channel_id=1, source_target_pairs={{0,3},{1,2},{2,1},{3,0},{4,7},{5,6},{6,5},{7,4},{8,11},{9,10},{10,... | collective-permute-start | bytes 73736 | tf_op jit(solution)/shard_map/ppermute | solution.py:285
  14.9 4.2 %collective-permute-start.6 = (f32[6,8,128]{2,1,0:T(8,128)S(1)}, f32[6,8,128]{2,1,0:T(8,128)S(1)}, u32[]{:S(2)}, u32[]{:S(2)}) collective-permute-start(f32[6,8,128]{2,1,0:T(8,128)S(1)} %shard_map.61.refs_0_), channel_id=1, source_target_pairs={{0,5},{1,4},{2,7},{3,6},{4,1},{5,0},{6,3},{7,2},{8,13},{9,12},{10,... | collective-permute-start | bytes 73736 | tf_op jit(solution)/shard_map/ppermute | solution.py:285
  17.6 4.2 %collective-permute-start.8 = (f32[6,8,128]{2,1,0:T(8,128)S(1)}, f32[6,8,128]{2,1,0:T(8,128)S(1)}, u32[]{:S(2)}, u32[]{:S(2)}) collective-permute-start(f32[6,8,128]{2,1,0:T(8,128)S(1)} %shard_map.61.refs_0_), channel_id=1, source_target_pairs={{0,7},{1,6},{2,5},{3,4},{4,3},{5,2},{6,1},{7,0},{8,15},{9,14},{10,... | collective-permute-start | bytes 73736 | tf_op jit(solution)/shard_map/ppermute | solution.py:285
  17.6 4.1 %collective-permute-start.3 = (f32[6,8,128]{2,1,0:T(8,128)S(1)}, f32[6,8,128]{2,1,0:T(8,128)S(1)}, u32[]{:S(2)}, u32[]{:S(2)}) collective-permute-start(f32[6,8,128]{2,1,0:T(8,128)S(1)} %shard_map.61.refs_0_), channel_id=1, source_target_pairs={{0,1},{1,0},{2,3},{3,2},{4,5},{5,4},{6,7},{7,6},{8,9},{9,8},{10,11... | collective-permute-start | bytes 73736 | tf_op jit(solution)/shard_map/ppermute | solution.py:288
  18.3 3.4 %collective-permute-start.5 = (f32[6,8,128]{2,1,0:T(8,128)S(1)}, f32[6,8,128]{2,1,0:T(8,128)S(1)}, u32[]{:S(2)}, u32[]{:S(2)}) collective-permute-start(f32[6,8,128]{2,1,0:T(8,128)S(1)} %collective-permute-done.4.refs_3_), channel_id=1, source_target_pairs={{0,1},{1,0},{2,3},{3,2},{4,5},{5,4},{6,7},{7,6},{8,9},{9,8},{10,11... | collective-permute-start | bytes 73736 | tf_op jit(solution)/shard_map/ppermute | solution.py:288
  19.1 2.6 %collective-permute-start.7 = (f32[6,8,128]{2,1,0:T(8,128)S(1)}, f32[6,8,128]{2,1,0:T(8,128)S(1)}, u32[]{:S(2)}, u32[]{:S(2)}) collective-permute-start(f32[6,8,128]{2,1,0:T(8,128)S(1)} %collective-permute-done.6.refs_5_), channel_id=1, source_target_pairs={{0,1},{1,0},{2,3},{3,2},{4,5},{5,4},{6,7},{7,6},{8,9},{9,8},{10,11... | collective-permute-start | bytes 73736 | tf_op jit(solution)/shard_map/ppermute | solution.py:288
  21.7 1.2 %collective-permute-start.9 = (f32[6,8,128]{2,1,0:T(8,128)S(1)}, f32[6,8,128]{2,1,0:T(8,128)S(1)}, u32[]{:S(2)}, u32[]{:S(2)}) collective-permute-start(f32[6,8,128]{2,1,0:T(8,128)S(1)} %collective-permute-done.8.refs_7_), channel_id=1, source_target_pairs={{0,1},{1,0},{2,3},{3,2},{4,5},{5,4},{6,7},{7,6},{8,9},{9,8},{10,11... | collective-permute-start | bytes 73736 | tf_op jit(solution)/shard_map/ppermute | solution.py:288
  23.6 4.5 %collective-permute-start.10 = (f32[3,8,128]{2,1,0:T(8,128)S(1)}, f32[3,8,128]{2,1,0:T(8,128)S(1)}, u32[]{:S(2)}, u32[]{:S(2)}) collective-permute-start(f32[3,8,128]{2,1,0:T(8,128)S(1)} %get-tuple-element.35), channel_id=1, source_target_pairs={{0,9},{1,8},{2,11},{3,10},{4,13},{5,12},{6,15},{7,14},{8,1},{9,0},... | collective-permute-start | bytes 36872 | tf_op jit(solution)/shard_map/ppermute | solution.py:304
  23.7 4.4 %collective-permute-start.11 = (f32[3,8,128]{2,1,0:T(8,128)S(1)}, f32[3,8,128]{2,1,0:T(8,128)S(1)}, u32[]{:S(2)}, u32[]{:S(2)}) collective-permute-start(f32[3,8,128]{2,1,0:T(8,128)S(1)} %get-tuple-element.35), channel_id=1, source_target_pairs={{0,17},{1,16},{2,19},{3,18},{4,21},{5,20},{6,23},{7,22},{8,25},{9,... | collective-permute-start | bytes 36872 | tf_op jit(solution)/shard_map/ppermute | solution.py:304
  25.7 4.9 %collective-permute-start.12 = (f32[3,8,128]{2,1,0:T(8,128)S(1)}, f32[3,8,128]{2,1,0:T(8,128)S(1)}, u32[]{:S(2)}, u32[]{:S(2)}) collective-permute-start(f32[3,8,128]{2,1,0:T(8,128)S(1)} %get-tuple-element.35), channel_id=1, source_target_pairs={{0,25},{1,24},{2,27},{3,26},{4,29},{5,28},{6,31},{7,30},{8,17},{9,... | collective-permute-start | bytes 36872 | tf_op jit(solution)/shard_map/ppermute | solution.py:304
  31.0 3.4 %collective-permute-start.14 = (f32[6,8,128]{2,1,0:T(8,128)S(1)}, f32[6,8,128]{2,1,0:T(8,128)S(1)}, u32[]{:S(2)}, u32[]{:S(2)}) collective-permute-start(f32[6,8,128]{2,1,0:T(8,128)S(1)} %shard_map.64.refs_0_), channel_id=1, source_target_pairs={{0,3},{1,2},{2,1},{3,0},{4,7},{5,6},{6,5},{7,4},{8,11},{9,10},{10,... | collective-permute-start | bytes 73736 | tf_op jit(solution)/shard_map/ppermute | solution.py:285
  31.5 3.3 %collective-permute-start.16 = (f32[6,8,128]{2,1,0:T(8,128)S(1)}, f32[6,8,128]{2,1,0:T(8,128)S(1)}, u32[]{:S(2)}, u32[]{:S(2)}) collective-permute-start(f32[6,8,128]{2,1,0:T(8,128)S(1)} %shard_map.64.refs_0_), channel_id=1, source_target_pairs={{0,5},{1,4},{2,7},{3,6},{4,1},{5,0},{6,3},{7,2},{8,13},{9,12},{10,... | collective-permute-start | bytes 73736 | tf_op jit(solution)/shard_map/ppermute | solution.py:285
  32.0 4.2 %collective-permute-start.18 = (f32[6,8,128]{2,1,0:T(8,128)S(1)}, f32[6,8,128]{2,1,0:T(8,128)S(1)}, u32[]{:S(2)}, u32[]{:S(2)}) collective-permute-start(f32[6,8,128]{2,1,0:T(8,128)S(1)} %shard_map.64.refs_0_), channel_id=1, source_target_pairs={{0,7},{1,6},{2,5},{3,4},{4,3},{5,2},{6,1},{7,0},{8,15},{9,14},{10,... | collective-permute-start | bytes 73736 | tf_op jit(solution)/shard_map/ppermute | solution.py:285
  34.0 2.3 %collective-permute-start.13 = (f32[6,8,128]{2,1,0:T(8,128)S(1)}, f32[6,8,128]{2,1,0:T(8,128)S(1)}, u32[]{:S(2)}, u32[]{:S(2)}) collective-permute-start(f32[6,8,128]{2,1,0:T(8,128)S(1)} %shard_map.64.refs_0_), channel_id=1, source_target_pairs={{0,1},{1,0},{2,3},{3,2},{4,5},{5,4},{6,7},{7,6},{8,9},{9,8},{10,11... | collective-permute-start | bytes 73736 | tf_op jit(solution)/shard_map/ppermute | solution.py:288
  34.4 1.9 %collective-permute-start.15 = (f32[6,8,128]{2,1,0:T(8,128)S(1)}, f32[6,8,128]{2,1,0:T(8,128)S(1)}, u32[]{:S(2)}, u32[]{:S(2)}) collective-permute-start(f32[6,8,128]{2,1,0:T(8,128)S(1)} %collective-permute-done.14.refs_3_), channel_id=1, source_target_pairs={{0,1},{1,0},{2,3},{3,2},{4,5},{5,4},{6,7},{7,6},{8,9},{9,8},{10,11... | collective-permute-start | bytes 73736 | tf_op jit(solution)/shard_map/ppermute | solution.py:288
  34.8 1.5 %collective-permute-start.17 = (f32[6,8,128]{2,1,0:T(8,128)S(1)}, f32[6,8,128]{2,1,0:T(8,128)S(1)}, u32[]{:S(2)}, u32[]{:S(2)}) collective-permute-start(f32[6,8,128]{2,1,0:T(8,128)S(1)} %collective-permute-done.16.refs_5_), channel_id=1, source_target_pairs={{0,1},{1,0},{2,3},{3,2},{4,5},{5,4},{6,7},{7,6},{8,9},{9,8},{10,11... | collective-permute-start | bytes 73736 | tf_op jit(solution)/shard_map/ppermute | solution.py:288
  36.1 1.2 %collective-permute-start.19 = (f32[6,8,128]{2,1,0:T(8,128)S(1)}, f32[6,8,128]{2,1,0:T(8,128)S(1)}, u32[]{:S(2)}, u32[]{:S(2)}) collective-permute-start(f32[6,8,128]{2,1,0:T(8,128)S(1)} %collective-permute-done.18.refs_7_), channel_id=1, source_target_pairs={{0,1},{1,0},{2,3},{3,2},{4,5},{5,4},{6,7},{7,6},{8,9},{9,8},{10,11... | collective-permute-start | bytes 73736 | tf_op jit(solution)/shard_map/ppermute | solution.py:288
  (1 other events, 0.7 us)
where the time goes:
time: 39.9 us; the launch traced here: 39.7 us
  starting transfers between devices  18 us (45%)
  waiting for transfers between devices  13.8 us (35%)
  Pallas kernels  5.43 us (14%)
  local copies, waits for them, and re-layouts  1.75 us (4%)
  between operations  0.76 us (2%)
    ppermute x6, starting transfers between devices, gather_tiles(): lax.ppermute(piece, 'tile', [(i, i ^ mask) for i in range(n)])  5.84 us
    ppermute x3, starting transfers between devices, exchange(): got.append(lax.ppermute(arrays[k - 1], 'survey', survey_pairs(k, n)))  5.71 us
    ppermute x3, waiting for transfers between devices, exchange(): got.append(lax.ppermute(arrays[k - 1], 'survey', survey_pairs(k, n)))  5.17 us
    ppermute x3, starting transfers between devices, exchange_across(): got.append(lax.ppermute(array, ('survey', 'tile'), pairs))  3.93 us
    ppermute x6, waiting for transfers between devices, gather_tiles(): lax.ppermute(piece, 'tile', [(i, i ^ mask) for i in range(n)])  3.84 us
    ppermute x3, waiting for transfers between devices, exchange_across(): got.append(lax.ppermute(array, ('survey', 'tile'), pairs))  2.55 us
    ppermute x8, starting transfers between devices, gather_tiles(): lax.ppermute(pieces[mask], 'tile', [(i, i ^ 1) for i in range(n)])  2.53 us
    pallas_call x1, Pallas kernels, local(): call(functools.partial(solve_last_kernel, masks), [field_shape, volume_sh...  2.41 us
  transfers between devices with their start and end apart: 20, of which 9 were waited for; matrix products, arithmetic and copies ran while one was open for 0% of the time, Pallas kernels for 4%

commit v1 on v0

--- a/solution.py
+++ b/solution.py
@@ -17,6 +17,7 @@
 bf16 = jnp.bfloat16
 VMEM = pl.BlockSpec(memory_space=pltpu.VMEM)
 ANY = pl.BlockSpec(memory_space=pl.ANY)
+HBM = pl.BlockSpec(memory_space=pltpu.HBM)
 PARAMS = pltpu.CompilerParams(vmem_limit_bytes=16 * 1024 * 1024)
 NT = (((1,), (1,)), ((), ()))
 
@@ -49,21 +50,32 @@
     return time_of(iota((samples, lanes), 0), samples)
 
 
-def joined_blocks(data_ref, start, rows_x, rows_y):
+def joined_blocks(data_ref, start):
+    rows_x, rows_y = data_ref.shape[1:3]
     block = start // rows_y
     split = start - block * rows_y
     after = jnp.minimum(block + 1, rows_x - 1)
-    here = data_ref[pl.ds(pl.multiple_of(block * rows_y, rows_y), rows_y), :].astype(f32)
-    there = data_ref[pl.ds(pl.multiple_of(after * rows_y, rows_y), rows_y), :].astype(f32)
+    here = data_ref[0, block].astype(f32)
+    there = data_ref[0, after].astype(f32)
     return jnp.where(iota(here.shape, 0) >= split, here, there).astype(data_ref.dtype)
 
 
-def pack_kernel(n, rows_x, index_ref, data_ref, *out_refs):
+def first_of(index_ref, source, destination):
+    return index_ref[source, 0, pl.ds(destination, 1), :][0, 0]
+
+
+def pack_kernel(n, index_hbm, data_hbm, *refs):
+    out_refs, (data_ref, index_ref, sems) = refs[: n - 1], refs[n - 1 :]
+    index_copy = pltpu.make_async_copy(index_hbm, index_ref, sems.at[0])
+    data_copy = pltpu.make_async_copy(data_hbm, data_ref, sems.at[1])
+    index_copy.start()
+    data_copy.start()
     me = lax.axis_index("survey")
-    rows_y = data_ref.shape[0] // rows_x
-    for k in range(1, n):
-        start = jnp.min(index_ref[me, pl.ds(receiver(me, k, n), 1), :])
-        out_refs[k - 1][...] = joined_blocks(data_ref, start, rows_x, rows_y)
+    index_copy.wait()
+    starts = [first_of(index_ref, me, receiver(me, k, n)) for k in range(1, n)]
+    data_copy.wait()
+    for out_ref, start in zip(out_refs, starts):
+        out_ref[...] = joined_blocks(data_ref, start)
 
 
 def put_rows(ref, k, rows):
@@ -83,7 +95,7 @@
 def prepare_kernel(n, index_ref, count_ref, data_ref, basis_ref, own_ref, moved_ref, mask_ref, energy_ref, slope_ref):
     me = lax.axis_index("survey")
     samples, rows_y = own_ref.shape[1:]
-    rows_x = data_ref.shape[0] // rows_y
+    rows_x = data_ref.shape[1]
     row, col = iota((samples, samples), 0), iota((samples, samples), 1)
     basis_ref[:samples, :] = jnp.where(row == col, 1.0, 0.0).astype(bf16)
     basis_ref[samples:, :] = (jnp.where(col == row + 1, 0.5, 0.0) - jnp.where(col == row - 1, 0.5, 0.0)).astype(bf16)
@@ -91,18 +103,18 @@
     position = iota((rows_x, rows_y), 0) * rows_y + iota((rows_x, rows_y), 1)
     for k in range(1, n):
         source = sender(me, k, n)
-        start = jnp.min(index_ref[source, pl.ds(me, 1), :])
+        start = first_of(index_ref, source, me)
         counts = count_ref[source]
         count = jnp.sum(jnp.where(iota(counts.shape, 1) == me, counts, 0))
         mask_ref[k - 1] = jnp.where((position >= start) & (position < start + count), 1.0, 0.0)
-        rows = joined_blocks(data_ref, start, rows_x, rows_y)
+        rows = joined_blocks(data_ref, start)
         both = lax.dot_general(basis_ref[...], rows, NT, preferred_element_type=f32)
         own_ref[k - 1] = both[:samples]
         moved_ref[k - 1] = both[samples:]
         put_rows(energy_ref, k - 1, energy_rows(both[:samples], both[samples:], time_pos))
     for x in range(rows_x):
         block = slice(x * rows_y, (x + 1) * rows_y)
-        slope_ref[block, :] = lax.dot_general(data_ref[block, :], basis_ref[samples:, :], NT, preferred_element_type=f32)
+        slope_ref[block, :] = lax.dot_general(data_ref[0, x], basis_ref[samples:, :], NT, preferred_element_type=f32)
 
 
 def corrected_lanes(values, moved, fields_ref, mask, time_pos):
@@ -244,15 +256,15 @@
 
 def solve_last_kernel(masks, smoothing_ref, before_ref, data_ref, slope_ref, *refs):
     pieces = refs[: len(masks)]
-    fields_ref, volume_ref, grid_ref, block_ref, sems = refs[len(masks) :]
+    fields_out, volume_ref, grid_ref, fields_ref, block_ref, sems = refs[len(masks) :]
     tile = lax.axis_index("tile")
     rows_x, rows_y = fields_ref.shape[1:]
-    samples = data_ref.shape[1]
+    samples = data_ref.shape[3]
     lanes = 16 * rows_x
     kind = iota((lanes, samples), 0) // rows_x
     time_pos = time_of(iota((lanes, samples), 1), samples)
     spread_power = jnp.where((kind >= 3) & (kind < 6), 1.0, jnp.where((kind >= 6) & (kind < 9), time_pos, 0.0))
-    spread_shift = jnp.where(kind < 3, 1.0, 0.0)
+    spread_shift = jnp.where(kind[:, :rows_y] < 3, 1.0, 0.0)
     spread = jnp.concatenate([spread_shift, spread_power], axis=1).astype(bf16)
     which = lax.rem(iota((rows_y, lanes), 1), rows_x)
     updates = grid_solve(masks, smoothing_ref, pieces, grid_ref, tile)
@@ -262,16 +274,17 @@
         mine = before_ref[c] + tile_part(grid_ref, c, tile, rows_x)
         fields_ref[c] = mine
         parts += three_parts(mine)
+    copies = [pltpu.make_async_copy(fields_ref, fields_out, sems.at[rows_x])]
+    copies[0].start()
     parts.append(jnp.zeros((lanes - 9 * rows_x, rows_y), f32))
     columns = jnp.transpose(jnp.concatenate(parts, axis=0))
-    copies = []
     for x in range(rows_x):
         rows = slice(x * rows_y, (x + 1) * rows_y)
         mine = jnp.where(which == x, columns, 0.0).astype(bf16)
         both = jnp.dot(mine, spread, preferred_element_type=f32)
-        shift, power = both[:, :samples], both[:, samples:]
-        moved = data_ref[rows, :].astype(f32) + shift * slope_ref[rows, :]
-        block_ref[rows, :] = (jnp.exp(power) * moved).astype(volume_ref.dtype)
+        shift = jnp.concatenate([both[:, :rows_y]] * (samples // rows_y), axis=1)
+        moved = data_ref[0, x].astype(f32) + shift * slope_ref[rows, :]
+        block_ref[rows, :] = (jnp.exp(both[:, rows_y:]) * moved).astype(volume_ref.dtype)
         copy = pltpu.make_async_copy(block_ref.at[rows, :], volume_ref.at[rows, :], sems.at[x])
         copy.start()
         copies.append(copy)
@@ -307,17 +320,15 @@
 
 def call(kernel, out_shape, n_in, **options):
     single = not isinstance(out_shape, list)
-    options = {"out_specs": VMEM if single else [VMEM] * len(out_shape), **options}
-    return pl.pallas_call(kernel, out_shape=out_shape, in_specs=[VMEM] * n_in, compiler_params=PARAMS, **options)
+    options = {"out_specs": VMEM if single else [VMEM] * len(out_shape), "in_specs": [VMEM] * n_in, **options}
+    return pl.pallas_call(kernel, out_shape=out_shape, compiler_params=PARAMS, **options)
 
 
 def local(n_survey, n_tile, data, correlation_index, correlation_count, smoothing):
     rows_x, rows_y, samples = data.shape[1:]
     total, cap = rows_x * rows_y, correlation_index.shape[-1]
-    assert cap <= rows_y and samples <= 256 and is_power(samples) and is_power(n_tile) and n_tile > 1
+    assert cap <= rows_y and samples % rows_y == 0 and samples <= 256 and is_power(samples) and is_power(n_tile) and n_tile > 1
     others = n_survey - 1
-    raw = data.reshape(total, samples)
-    index = correlation_index[:, 0]
     smoothing = smoothing.reshape(1, 3)
     packed = jax.ShapeDtypeStruct((rows_y, samples), data.dtype)
     field_shape = jax.ShapeDtypeStruct((3, rows_x, rows_y), f32)
@@ -330,13 +341,19 @@
     volume_shape = jax.ShapeDtypeStruct((total, samples), data.dtype)
     grid = pltpu.VMEM((6, rows_x * n_tile, rows_y), f32)
 
-    outgoing = call(functools.partial(pack_kernel, n_survey, rows_x), [packed] * others, 2)(index, raw)
+    *outgoing, data = call(
+        functools.partial(pack_kernel, n_survey),
+        [packed] * others + [jax.ShapeDtypeStruct(data.shape, data.dtype)],
+        2,
+        in_specs=[HBM] * 2,
+        scratch_shapes=[pltpu.VMEM(correlation_index.shape, jnp.int32), pltpu.SemaphoreType.DMA((2,))],
+    )(*[pltpu.with_memory_space_constraint(a, pltpu.HBM) for a in (correlation_index, data)])
     arrived = exchange(outgoing, n_survey)
     basis, own, moved, mask, energy, slope = call(
         functools.partial(prepare_kernel, n_survey),
         [basis_shape, lane_shape, lane_shape, mask_shape, energy_shape, slope_shape],
         3,
-    )(index, correlation_count, raw)
+    )(correlation_index, correlation_count, data)
     terms = call(functools.partial(pair_first_kernel, n_survey), term_shape, 5 + others)(
         basis, own, moved, mask, energy, *arrived
     )
@@ -359,9 +376,14 @@
         functools.partial(solve_last_kernel, masks),
         [field_shape, volume_shape],
         4 + n_tile,
-        out_specs=[VMEM, ANY],
-        scratch_shapes=[grid, pltpu.VMEM((total, samples), data.dtype), pltpu.SemaphoreType.DMA((rows_x,))],
-    )(smoothing, fields, raw, slope, *pieces)
+        out_specs=[ANY, ANY],
+        scratch_shapes=[
+            grid,
+            pltpu.VMEM((3, rows_x, rows_y), f32),
+            pltpu.VMEM((total, samples), data.dtype),
+            pltpu.SemaphoreType.DMA((rows_x + 1,)),
+        ],
+    )(smoothing, fields, data, slope, *pieces)
     return fields.reshape(1, 3, rows_x, rows_y), volume.reshape(1, rows_x, rows_y, samples)
 
 

time: 39.9 us -> 38.4 us (0.962)
  local copies, waits for them, and re-layouts: 1.75 us -> 0.01 us
    unnamed x10 -> x6, local copies, waits for them, and re-layouts: 1.75 us -> 0.01 us
    pallas_call x1, Pallas kernels: 0.27 us -> 1.14 us  [local(): call(functools.partial(pack_kernel, n_survey), [packed] * others + [jax.S...]
    pallas_call x1, Pallas kernels: 2.41 us -> 1.79 us  [local(): call(functools.partial(solve_last_kernel, masks), [field_shape, volume_sh...]
  transfers between devices with their start and end apart: 20 -> 20, of which waited for: 9 -> 9; matrix products, arithmetic and copies ran while one was open for 0% -> 0% of each run, Pallas kernels for 4% -> 3%
where the time goes in v1:
time: 38.4 us; the launch traced here: 38.2 us
  starting transfers between devices  18 us (47%)
  waiting for transfers between devices  13.9 us (36%)
  Pallas kernels  5.59 us (15%)
  between operations  0.75 us (2%)
    ppermute x6, starting transfers between devices, gather_tiles(): lax.ppermute(piece, 'tile', [(i, i ^ mask) for i in range(n)])  5.84 us
    ppermute x3, starting transfers between devices, exchange(): got.append(lax.ppermute(arrays[k - 1], 'survey', survey_pairs(k, n)))  5.71 us
    ppermute x3, waiting for transfers between devices, exchange(): got.append(lax.ppermute(arrays[k - 1], 'survey', survey_pairs(k, n)))  5.27 us
    ppermute x3, starting transfers between devices, exchange_across(): got.append(lax.ppermute(array, ('survey', 'tile'), pairs))  3.93 us
    ppermute x6, waiting for transfers between devices, gather_tiles(): lax.ppermute(piece, 'tile', [(i, i ^ mask) for i in range(n)])  3.84 us
    ppermute x3, waiting for transfers between devices, exchange_across(): got.append(lax.ppermute(array, ('survey', 'tile'), pairs))  2.55 us
    ppermute x8, starting transfers between devices, gather_tiles(): lax.ppermute(pieces[mask], 'tile', [(i, i ^ 1) for i in range(n)])  2.54 us
    ppermute x8, waiting for transfers between devices, gather_tiles(): lax.ppermute(pieces[mask], 'tile', [(i, i ^ 1) for i in range(n)])  2.21 us
  transfers between devices with their start and end apart: 20, of which 9 were waited for; matrix products, arithmetic and copies ran while one was open for 0% of the time, Pallas kernels for 3%

profile of v1, /device:TPU:0, one launch (start us, length us, event | category | flops | bytes accessed | tf_op | source)
XLA Modules:
  0.0 38.2 jit_solution(2606628670757600377)
XLA Ops:
  0.6 1.1 %shard_map.59 = (bf16[128,256]{1,0:T(8,128)(2,1)S(1)}, bf16[128,256]{1,0:T(8,128)(2,1)S(1)}, bf16[128,256]{1,0:T(8,128)(2,1)S(1)}, bf16[1,8,128,256]{3,2,1,0:T(8,128)(2,1)S(1)}) custom-call(s32[4,1,4,128]{3,2,1,0:T(4,128)} %index_ref.1, bf16[1,8,128,256]{3,2,1,0:T(8,128)(2,1)} %data_hbm.1), custom_call_target="tpu_custom_call" | custom-call | tf_op jit(solution)/shard_map/pallas_call | solution.py:344
  1.8 3.1 %collective-permute-start = (bf16[128,256]{1,0:T(8,128)(2,1)S(1)}, bf16[128,256]{1,0:T(8,128)(2,1)S(1)}, u32[]{:S(2)}, u32[]{:S(2)}) collective-permute-start(bf16[128,256]{1,0:T(8,128)(2,1)S(1)} %get-tuple-element.27), channel_id=1, source_target_pairs={{0,8},{8,0},{16,24},{24,16},{1,9},{9,1},{17,25},{25,17},{2,10},{10... | collective-permute-start | bytes 196616 | tf_op jit(solution)/shard_map/ppermute | solution.py:309
  4.9 2.6 %collective-permute-start.1 = (bf16[128,256]{1,0:T(8,128)(2,1)S(1)}, bf16[128,256]{1,0:T(8,128)(2,1)S(1)}, u32[]{:S(2)}, u32[]{:S(2)}) collective-permute-start(bf16[128,256]{1,0:T(8,128)(2,1)S(1)} %get-tuple-element.28), channel_id=1, source_target_pairs={{0,16},{8,24},{16,0},{24,8},{1,17},{9,25},{17,1},{25,9},{2,18},{10... | collective-permute-start | bytes 196616 | tf_op jit(solution)/shard_map/ppermute | solution.py:309
  7.5 0.8 %shard_map.60 = (bf16[512,256]{1,0:T(8,128)(2,1)S(1)}, f32[3,256,128]{2,1,0:T(8,128)S(1)}, f32[3,256,128]{2,1,0:T(8,128)S(1)}, f32[3,8,128]{2,1,0:T(8,128)S(1)},...) custom-call(s32[4,1,4,128]{3,2,1,0:T(4,128)S(1)} %copy-done, s32[4,1,4]{2,1,0:T(1,128)S(1)} %copy-done.1, ...), custom_call_target="tpu_custom_call" | custom-call | tf_op jit(solution)/shard_map/pallas_call | solution.py:352
  8.3 3.9 %collective-permute-done.1.refs_1_ = bf16[128,256]{1,0:T(8,128)(2,1)S(1)} collective-permute-done((bf16[128,256]{1,0:T(8,128)(2,1)S(1)}, bf16[128,256]{1,0:T(8,128)(2,1)S(1)}, u32[]{:S(2)}, u32[]{:S(2)}) %collective-permute-start.1) | collective-permute-done | bytes 65568 | tf_op jit(solution)/shard_map/ppermute | solution.py:309
  12.2 1.4 %collective-permute-done.2.refs_2_ = bf16[128,256]{1,0:T(8,128)(2,1)S(1)} collective-permute-done((bf16[128,256]{1,0:T(8,128)(2,1)S(1)}, bf16[128,256]{1,0:T(8,128)(2,1)S(1)}, u32[]{:S(2)}, u32[]{:S(2)}) %collective-permute-start.2) | collective-permute-done | bytes 65568 | tf_op jit(solution)/shard_map/ppermute | solution.py:309
  14.0 2.7 %collective-permute-start.6 = (f32[6,8,128]{2,1,0:T(8,128)S(1)}, f32[6,8,128]{2,1,0:T(8,128)S(1)}, u32[]{:S(2)}, u32[]{:S(2)}) collective-permute-start(f32[6,8,128]{2,1,0:T(8,128)S(1)} %shard_map.61.refs_0_), channel_id=1, source_target_pairs={{0,5},{1,4},{2,7},{3,6},{4,1},{5,0},{6,3},{7,2},{8,13},{9,12},{10,... | collective-permute-start | bytes 73736 | tf_op jit(solution)/shard_map/ppermute | solution.py:298
  16.7 0.6 %collective-permute-start.3 = (f32[6,8,128]{2,1,0:T(8,128)S(1)}, f32[6,8,128]{2,1,0:T(8,128)S(1)}, u32[]{:S(2)}, u32[]{:S(2)}) collective-permute-start(f32[6,8,128]{2,1,0:T(8,128)S(1)} %shard_map.61.refs_0_), channel_id=1, source_target_pairs={{0,1},{1,0},{2,3},{3,2},{4,5},{5,4},{6,7},{7,6},{8,9},{9,8},{10,11... | collective-permute-start | bytes 73736 | tf_op jit(solution)/shard_map/ppermute | solution.py:301
  17.6 0.7 %collective-permute-done.6.refs_5_ = f32[6,8,128]{2,1,0:T(8,128)S(1)} collective-permute-done((f32[6,8,128]{2,1,0:T(8,128)S(1)}, f32[6,8,128]{2,1,0:T(8,128)S(1)}, u32[]{:S(2)}, u32[]{:S(2)}) %collective-permute-start.6) | collective-permute-done | bytes 24608 | tf_op jit(solution)/shard_map/ppermute | solution.py:298
  18.2 0.6 %collective-permute-start.7 = (f32[6,8,128]{2,1,0:T(8,128)S(1)}, f32[6,8,128]{2,1,0:T(8,128)S(1)}, u32[]{:S(2)}, u32[]{:S(2)}) collective-permute-start(f32[6,8,128]{2,1,0:T(8,128)S(1)} %collective-permute-done.6.refs_5_), channel_id=1, source_target_pairs={{0,1},{1,0},{2,3},{3,2},{4,5},{5,4},{6,7},{7,6},{8,9},{9,8},{10,11... | collective-permute-start | bytes 73736 | tf_op jit(solution)/shard_map/ppermute | solution.py:301
  18.9 2.0 %collective-permute-done.8.refs_7_ = f32[6,8,128]{2,1,0:T(8,128)S(1)} collective-permute-done((f32[6,8,128]{2,1,0:T(8,128)S(1)}, f32[6,8,128]{2,1,0:T(8,128)S(1)}, u32[]{:S(2)}, u32[]{:S(2)}) %collective-permute-start.8) | collective-permute-done | bytes 24608 | tf_op jit(solution)/shard_map/ppermute | solution.py:298
  20.9 1.2 %collective-permute-done.9.refs_6_ = f32[6,8,128]{2,1,0:T(8,128)S(1)} collective-permute-done((f32[6,8,128]{2,1,0:T(8,128)S(1)}, f32[6,8,128]{2,1,0:T(8,128)S(1)}, u32[]{:S(2)}, u32[]{:S(2)}) %collective-permute-start.9) | collective-permute-done | bytes 24608 | tf_op jit(solution)/shard_map/ppermute | solution.py:301
  22.1 0.6 %shard_map.62 = (f32[3,8,128]{2,1,0:T(8,128)S(1)}, f32[3,8,128]{2,1,0:T(8,128)S(1)}) custom-call(f32[1,3]{1,0:T(1,128)S(1)} %bitcast.3, f32[6,8,128]{2,1,0:T(8,128)S(1)} %shard_map.61.refs_0_, f32[6,8,128]{2,1,0:T(8,128)S(1)} %collective-permute-done.3.refs_1_, f32[6,8,128]{2,1,0:T(8,128)S(1)} %collective-permute-done.5.refs_2_, ...), custom_call_target="tpu_custom_call" | custom-call | tf_op jit(solution)/shard_map/pallas_call | solution.py:361
  22.8 2.0 %collective-permute-start.11 = (f32[3,8,128]{2,1,0:T(8,128)S(1)}, f32[3,8,128]{2,1,0:T(8,128)S(1)}, u32[]{:S(2)}, u32[]{:S(2)}) collective-permute-start(f32[3,8,128]{2,1,0:T(8,128)S(1)} %get-tuple-element.37), channel_id=1, source_target_pairs={{0,17},{1,16},{2,19},{3,18},{4,21},{5,20},{6,23},{7,22},{8,25},{9,... | collective-permute-start | bytes 36872 | tf_op jit(solution)/shard_map/ppermute | solution.py:317
  24.8 1.8 %collective-permute-start.12 = (f32[3,8,128]{2,1,0:T(8,128)S(1)}, f32[3,8,128]{2,1,0:T(8,128)S(1)}, u32[]{:S(2)}, u32[]{:S(2)}) collective-permute-start(f32[3,8,128]{2,1,0:T(8,128)S(1)} %get-tuple-element.37), channel_id=1, source_target_pairs={{0,25},{1,24},{2,27},{3,26},{4,29},{5,28},{6,31},{7,30},{8,17},{9,... | collective-permute-start | bytes 36872 | tf_op jit(solution)/shard_map/ppermute | solution.py:317
  26.7 0.5 %shard_map.63 = (f32[3,256,128]{2,1,0:T(8,128)S(1)}, f32[3,256,128]{2,1,0:T(8,128)S(1)}, f32[3,8,128]{2,1,0:T(8,128)S(1)}, f32[3,256,128]{2,1,0:T(8,128)S(1)}, f32[3,256,128]{2,1,0:T(8,128)S(1)}) custom-call(f32[3,8,128]{2,1,0:T(8,128)S(1)} %get-tuple-element.30.fields_ref.before_ref, bf16[512,256]{1,0:T(8,128)(2,1)S(1)} %get-tuple-element.22.basis_ref, ...), custom_call_target="tpu_custom_call" | custom-call | tf_op jit(solution)/shard_map/pallas_call | solution.py:366
  27.2 2.5 %collective-permute-done.12.refs_2_ = f32[3,8,128]{2,1,0:T(8,128)S(1)} collective-permute-done((f32[3,8,128]{2,1,0:T(8,128)S(1)}, f32[3,8,128]{2,1,0:T(8,128)S(1)}, u32[]{:S(2)}, u32[]{:S(2)}) %collective-permute-start.12) | collective-permute-done | bytes 12320 | tf_op jit(solution)/shard_map/ppermute | solution.py:317
  30.1 0.5 %collective-permute-start.14 = (f32[6,8,128]{2,1,0:T(8,128)S(1)}, f32[6,8,128]{2,1,0:T(8,128)S(1)}, u32[]{:S(2)}, u32[]{:S(2)}) collective-permute-start(f32[6,8,128]{2,1,0:T(8,128)S(1)} %shard_map.64.refs_0_), channel_id=1, source_target_pairs={{0,3},{1,2},{2,1},{3,0},{4,7},{5,6},{6,5},{7,4},{8,11},{9,10},{10,... | collective-permute-start | bytes 73736 | tf_op jit(solution)/shard_map/ppermute | solution.py:298
  30.7 0.5 %collective-permute-start.16 = (f32[6,8,128]{2,1,0:T(8,128)S(1)}, f32[6,8,128]{2,1,0:T(8,128)S(1)}, u32[]{:S(2)}, u32[]{:S(2)}) collective-permute-start(f32[6,8,128]{2,1,0:T(8,128)S(1)} %shard_map.64.refs_0_), channel_id=1, source_target_pairs={{0,5},{1,4},{2,7},{3,6},{4,1},{5,0},{6,3},{7,2},{8,13},{9,12},{10,... | collective-permute-start | bytes 73736 | tf_op jit(solution)/shard_map/ppermute | solution.py:298
  31.1 2.1 %collective-permute-start.18 = (f32[6,8,128]{2,1,0:T(8,128)S(1)}, f32[6,8,128]{2,1,0:T(8,128)S(1)}, u32[]{:S(2)}, u32[]{:S(2)}) collective-permute-start(f32[6,8,128]{2,1,0:T(8,128)S(1)} %shard_map.64.refs_0_), channel_id=1, source_target_pairs={{0,7},{1,6},{2,5},{3,4},{4,3},{5,2},{6,1},{7,0},{8,15},{9,14},{10,... | collective-permute-start | bytes 73736 | tf_op jit(solution)/shard_map/ppermute | solution.py:298
  33.5 0.4 %collective-permute-start.15 = (f32[6,8,128]{2,1,0:T(8,128)S(1)}, f32[6,8,128]{2,1,0:T(8,128)S(1)}, u32[]{:S(2)}, u32[]{:S(2)}) collective-permute-start(f32[6,8,128]{2,1,0:T(8,128)S(1)} %collective-permute-done.14.refs_3_), channel_id=1, source_target_pairs={{0,1},{1,0},{2,3},{3,2},{4,5},{5,4},{6,7},{7,6},{8,9},{9,8},{10,11... | collective-permute-start | bytes 73736 | tf_op jit(solution)/shard_map/ppermute | solution.py:301
  34.3 1.0 %collective-permute-done.18.refs_7_ = f32[6,8,128]{2,1,0:T(8,128)S(1)} collective-permute-done((f32[6,8,128]{2,1,0:T(8,128)S(1)}, f32[6,8,128]{2,1,0:T(8,128)S(1)}, u32[]{:S(2)}, u32[]{:S(2)}) %collective-permute-start.18) | collective-permute-done | bytes 24608 | tf_op jit(solution)/shard_map/ppermute | solution.py:298
  35.4 1.0 %collective-permute-done.19.refs_6_ = f32[6,8,128]{2,1,0:T(8,128)S(1)} collective-permute-done((f32[6,8,128]{2,1,0:T(8,128)S(1)}, f32[6,8,128]{2,1,0:T(8,128)S(1)}, u32[]{:S(2)}, u32[]{:S(2)}) %collective-permute-start.19) | collective-permute-done | bytes 24608 | tf_op jit(solution)/shard_map/ppermute | solution.py:301
  36.5 1.8 %shard_map.65 = (f32[3,8,128]{2,1,0:T(8,128)}, bf16[1024,256]{1,0:T(8,128)(2,1)}) custom-call(f32[1,3]{1,0:T(1,128)S(1)} %bitcast.4, f32[3,8,128]{2,1,0:T(8,128)S(1)} %get-tuple-element.30.fields_ref.before_ref, bf16[1,8,128,256]{3,2,1,0:T(8,128)(2,1)S(1)} %get-tuple-element.21.data_ref, f32[1024,256]{1,0:T(8,128)S(1)} %get-tuple-element.31.slope_ref, ...), custom_call_target="tpu_custom_call" | custom-call | tf_op jit(solution)/shard_map/pallas_call | solution.py:375
  (29 shorter events, 2.0 us)
Async XLA Ops:
  0.6 6.9 %copy-start = (s32[4,1,4,128]{3,2,1,0:T(4,128)S(1)}, s32[4,1,4,128]{3,2,1,0:T(4,128)}, u32[]{:S(2)}) copy-start(s32[4,1,4,128]{3,2,1,0:T(4,128)} %index_ref.1) | copy-start | bytes 24580
  1.8 6.5 %collective-permute-start = (bf16[128,256]{1,0:T(8,128)(2,1)S(1)}, bf16[128,256]{1,0:T(8,128)(2,1)S(1)}, u32[]{:S(2)}, u32[]{:S(2)}) collective-permute-start(bf16[128,256]{1,0:T(8,128)(2,1)S(1)} %get-tuple-element.27), channel_id=1, source_target_pairs={{0,8},{8,0},{16,24},{24,16},{1,9},{9,1},{17,25},{25,17},{2,10},{10... | collective-permute-start | bytes 196616 | tf_op jit(solution)/shard_map/ppermute | solution.py:309
  4.9 2.6 %copy-start.1 = (s32[4,1,4]{2,1,0:T(1,128)S(1)}, s32[4,1,4]{2,1,0:T(1,128)}, u32[]{:S(2)}) copy-start(s32[4,1,4]{2,1,0:T(1,128)} %count_ref.1) | copy-start | bytes 196
  4.9 7.3 %collective-permute-start.1 = (bf16[128,256]{1,0:T(8,128)(2,1)S(1)}, bf16[128,256]{1,0:T(8,128)(2,1)S(1)}, u32[]{:S(2)}, u32[]{:S(2)}) collective-permute-start(bf16[128,256]{1,0:T(8,128)(2,1)S(1)} %get-tuple-element.28), channel_id=1, source_target_pairs={{0,16},{8,24},{16,0},{24,8},{1,17},{9,25},{17,1},{25,9},{2,18},{10... | collective-permute-start | bytes 196616 | tf_op jit(solution)/shard_map/ppermute | solution.py:309
  7.5 6.1 %collective-permute-start.2 = (bf16[128,256]{1,0:T(8,128)(2,1)S(1)}, bf16[128,256]{1,0:T(8,128)(2,1)S(1)}, u32[]{:S(2)}, u32[]{:S(2)}) collective-permute-start(bf16[128,256]{1,0:T(8,128)(2,1)S(1)} %get-tuple-element.29), channel_id=1, source_target_pairs={{0,24},{8,16},{16,8},{24,0},{1,25},{9,17},{17,9},{25,1},{2,26},{10... | collective-permute-start | bytes 196616 | tf_op jit(solution)/shard_map/ppermute | solution.py:309
  13.9 8.2 %copy-start.2 = (f32[3]{0:T(128)S(1)}, f32[3]{0:T(128)}, u32[]{:S(2)}) copy-start(f32[3]{0:T(128)} %param.7) | copy-start | bytes 40
  13.9 3.5 %collective-permute-start.4 = (f32[6,8,128]{2,1,0:T(8,128)S(1)}, f32[6,8,128]{2,1,0:T(8,128)S(1)}, u32[]{:S(2)}, u32[]{:S(2)}) collective-permute-start(f32[6,8,128]{2,1,0:T(8,128)S(1)} %shard_map.61.refs_0_), channel_id=1, source_target_pairs={{0,3},{1,2},{2,1},{3,0},{4,7},{5,6},{6,5},{7,4},{8,11},{9,10},{10,... | collective-permute-start | bytes 73736 | tf_op jit(solution)/shard_map/ppermute | solution.py:298
  14.0 4.2 %collective-permute-start.6 = (f32[6,8,128]{2,1,0:T(8,128)S(1)}, f32[6,8,128]{2,1,0:T(8,128)S(1)}, u32[]{:S(2)}, u32[]{:S(2)}) collective-permute-start(f32[6,8,128]{2,1,0:T(8,128)S(1)} %shard_map.61.refs_0_), channel_id=1, source_target_pairs={{0,5},{1,4},{2,7},{3,6},{4,1},{5,0},{6,3},{7,2},{8,13},{9,12},{10,... | collective-permute-start | bytes 73736 | tf_op jit(solution)/shard_map/ppermute | solution.py:298
  16.7 4.2 %collective-permute-start.8 = (f32[6,8,128]{2,1,0:T(8,128)S(1)}, f32[6,8,128]{2,1,0:T(8,128)S(1)}, u32[]{:S(2)}, u32[]{:S(2)}) collective-permute-start(f32[6,8,128]{2,1,0:T(8,128)S(1)} %shard_map.61.refs_0_), channel_id=1, source_target_pairs={{0,7},{1,6},{2,5},{3,4},{4,3},{5,2},{6,1},{7,0},{8,15},{9,14},{10,... | collective-permute-start | bytes 73736 | tf_op jit(solution)/shard_map/ppermute | solution.py:298
  16.7 4.1 %collective-permute-start.3 = (f32[6,8,128]{2,1,0:T(8,128)S(1)}, f32[6,8,128]{2,1,0:T(8,128)S(1)}, u32[]{:S(2)}, u32[]{:S(2)}) collective-permute-start(f32[6,8,128]{2,1,0:T(8,128)S(1)} %shard_map.61.refs_0_), channel_id=1, source_target_pairs={{0,1},{1,0},{2,3},{3,2},{4,5},{5,4},{6,7},{7,6},{8,9},{9,8},{10,11... | collective-permute-start | bytes 73736 | tf_op jit(solution)/shard_map/ppermute | solution.py:301
  17.5 3.4 %collective-permute-start.5 = (f32[6,8,128]{2,1,0:T(8,128)S(1)}, f32[6,8,128]{2,1,0:T(8,128)S(1)}, u32[]{:S(2)}, u32[]{:S(2)}) collective-permute-start(f32[6,8,128]{2,1,0:T(8,128)S(1)} %collective-permute-done.4.refs_3_), channel_id=1, source_target_pairs={{0,1},{1,0},{2,3},{3,2},{4,5},{5,4},{6,7},{7,6},{8,9},{9,8},{10,11... | collective-permute-start | bytes 73736 | tf_op jit(solution)/shard_map/ppermute | solution.py:301
  18.2 2.6 %collective-permute-start.7 = (f32[6,8,128]{2,1,0:T(8,128)S(1)}, f32[6,8,128]{2,1,0:T(8,128)S(1)}, u32[]{:S(2)}, u32[]{:S(2)}) collective-permute-start(f32[6,8,128]{2,1,0:T(8,128)S(1)} %collective-permute-done.6.refs_5_), channel_id=1, source_target_pairs={{0,1},{1,0},{2,3},{3,2},{4,5},{5,4},{6,7},{7,6},{8,9},{9,8},{10,11... | collective-permute-start | bytes 73736 | tf_op jit(solution)/shard_map/ppermute | solution.py:301
  20.9 1.2 %collective-permute-start.9 = (f32[6,8,128]{2,1,0:T(8,128)S(1)}, f32[6,8,128]{2,1,0:T(8,128)S(1)}, u32[]{:S(2)}, u32[]{:S(2)}) collective-permute-start(f32[6,8,128]{2,1,0:T(8,128)S(1)} %collective-permute-done.8.refs_7_), channel_id=1, source_target_pairs={{0,1},{1,0},{2,3},{3,2},{4,5},{5,4},{6,7},{7,6},{8,9},{9,8},{10,11... | collective-permute-start | bytes 73736 | tf_op jit(solution)/shard_map/ppermute | solution.py:301
  22.7 4.5 %collective-permute-start.10 = (f32[3,8,128]{2,1,0:T(8,128)S(1)}, f32[3,8,128]{2,1,0:T(8,128)S(1)}, u32[]{:S(2)}, u32[]{:S(2)}) collective-permute-start(f32[3,8,128]{2,1,0:T(8,128)S(1)} %get-tuple-element.37), channel_id=1, source_target_pairs={{0,9},{1,8},{2,11},{3,10},{4,13},{5,12},{6,15},{7,14},{8,1},{9,0},... | collective-permute-start | bytes 36872 | tf_op jit(solution)/shard_map/ppermute | solution.py:317
  22.8 4.4 %collective-permute-start.11 = (f32[3,8,128]{2,1,0:T(8,128)S(1)}, f32[3,8,128]{2,1,0:T(8,128)S(1)}, u32[]{:S(2)}, u32[]{:S(2)}) collective-permute-start(f32[3,8,128]{2,1,0:T(8,128)S(1)} %get-tuple-element.37), channel_id=1, source_target_pairs={{0,17},{1,16},{2,19},{3,18},{4,21},{5,20},{6,23},{7,22},{8,25},{9,... | collective-permute-start | bytes 36872 | tf_op jit(solution)/shard_map/ppermute | solution.py:317
  24.8 4.9 %collective-permute-start.12 = (f32[3,8,128]{2,1,0:T(8,128)S(1)}, f32[3,8,128]{2,1,0:T(8,128)S(1)}, u32[]{:S(2)}, u32[]{:S(2)}) collective-permute-start(f32[3,8,128]{2,1,0:T(8,128)S(1)} %get-tuple-element.37), channel_id=1, source_target_pairs={{0,25},{1,24},{2,27},{3,26},{4,29},{5,28},{6,31},{7,30},{8,17},{9,... | collective-permute-start | bytes 36872 | tf_op jit(solution)/shard_map/ppermute | solution.py:317
  30.1 3.4 %collective-permute-start.14 = (f32[6,8,128]{2,1,0:T(8,128)S(1)}, f32[6,8,128]{2,1,0:T(8,128)S(1)}, u32[]{:S(2)}, u32[]{:S(2)}) collective-permute-start(f32[6,8,128]{2,1,0:T(8,128)S(1)} %shard_map.64.refs_0_), channel_id=1, source_target_pairs={{0,3},{1,2},{2,1},{3,0},{4,7},{5,6},{6,5},{7,4},{8,11},{9,10},{10,... | collective-permute-start | bytes 73736 | tf_op jit(solution)/shard_map/ppermute | solution.py:298
  30.7 3.3 %collective-permute-start.16 = (f32[6,8,128]{2,1,0:T(8,128)S(1)}, f32[6,8,128]{2,1,0:T(8,128)S(1)}, u32[]{:S(2)}, u32[]{:S(2)}) collective-permute-start(f32[6,8,128]{2,1,0:T(8,128)S(1)} %shard_map.64.refs_0_), channel_id=1, source_target_pairs={{0,5},{1,4},{2,7},{3,6},{4,1},{5,0},{6,3},{7,2},{8,13},{9,12},{10,... | collective-permute-start | bytes 73736 | tf_op jit(solution)/shard_map/ppermute | solution.py:298
  31.1 4.2 %collective-permute-start.18 = (f32[6,8,128]{2,1,0:T(8,128)S(1)}, f32[6,8,128]{2,1,0:T(8,128)S(1)}, u32[]{:S(2)}, u32[]{:S(2)}) collective-permute-start(f32[6,8,128]{2,1,0:T(8,128)S(1)} %shard_map.64.refs_0_), channel_id=1, source_target_pairs={{0,7},{1,6},{2,5},{3,4},{4,3},{5,2},{6,1},{7,0},{8,15},{9,14},{10,... | collective-permute-start | bytes 73736 | tf_op jit(solution)/shard_map/ppermute | solution.py:298
  33.2 2.3 %collective-permute-start.13 = (f32[6,8,128]{2,1,0:T(8,128)S(1)}, f32[6,8,128]{2,1,0:T(8,128)S(1)}, u32[]{:S(2)}, u32[]{:S(2)}) collective-permute-start(f32[6,8,128]{2,1,0:T(8,128)S(1)} %shard_map.64.refs_0_), channel_id=1, source_target_pairs={{0,1},{1,0},{2,3},{3,2},{4,5},{5,4},{6,7},{7,6},{8,9},{9,8},{10,11... | collective-permute-start | bytes 73736 | tf_op jit(solution)/shard_map/ppermute | solution.py:301
  33.5 1.9 %collective-permute-start.15 = (f32[6,8,128]{2,1,0:T(8,128)S(1)}, f32[6,8,128]{2,1,0:T(8,128)S(1)}, u32[]{:S(2)}, u32[]{:S(2)}) collective-permute-start(f32[6,8,128]{2,1,0:T(8,128)S(1)} %collective-permute-done.14.refs_3_), channel_id=1, source_target_pairs={{0,1},{1,0},{2,3},{3,2},{4,5},{5,4},{6,7},{7,6},{8,9},{9,8},{10,11... | collective-permute-start | bytes 73736 | tf_op jit(solution)/shard_map/ppermute | solution.py:301
  33.9 1.5 %collective-permute-start.17 = (f32[6,8,128]{2,1,0:T(8,128)S(1)}, f32[6,8,128]{2,1,0:T(8,128)S(1)}, u32[]{:S(2)}, u32[]{:S(2)}) collective-permute-start(f32[6,8,128]{2,1,0:T(8,128)S(1)} %collective-permute-done.16.refs_5_), channel_id=1, source_target_pairs={{0,1},{1,0},{2,3},{3,2},{4,5},{5,4},{6,7},{7,6},{8,9},{9,8},{10,11... | collective-permute-start | bytes 73736 | tf_op jit(solution)/shard_map/ppermute | solution.py:301
  35.3 1.2 %collective-permute-start.19 = (f32[6,8,128]{2,1,0:T(8,128)S(1)}, f32[6,8,128]{2,1,0:T(8,128)S(1)}, u32[]{:S(2)}, u32[]{:S(2)}) collective-permute-start(f32[6,8,128]{2,1,0:T(8,128)S(1)} %collective-permute-done.18.refs_7_), channel_id=1, source_target_pairs={{0,1},{1,0},{2,3},{3,2},{4,5},{5,4},{6,7},{7,6},{8,9},{9,8},{10,11... | collective-permute-start | bytes 73736 | tf_op jit(solution)/shard_map/ppermute | solution.py:301

commit v2 on v1

--- a/solution.py
+++ b/solution.py
@@ -210,23 +210,31 @@
 
     residual = [grid_ref[c] for c in each]
     image = apply(residual)
-    norm_now = [total(residual[c] * residual[c]) for c in each]
-    product = [total(residual[c] * image[c]) for c in each]
-    alpha = [norm_now[c] / product[c] for c in each]
-    direction, along = residual, image
-    update = [alpha[c] * direction[c] for c in each]
-    for iteration in range(1, CG_ITERS):
-        residual = [residual[c] - alpha[c] * along[c] for c in each]
-        image = apply(residual)
-        norm_next = [total(residual[c] * residual[c]) for c in each]
+    norm_before, alpha = [None] * 3, [None] * 3
+    direction, along, beyond, update = [None] * 3, [None] * 3, [None] * 3, [None] * 3
+    for iteration in range(CG_ITERS):
+        last = iteration + 1 == CG_ITERS
+        norm_now = [total(residual[c] * residual[c]) for c in each]
         product = [total(residual[c] * image[c]) for c in each]
-        ratio = [norm_next[c] / norm_now[c] for c in each]
-        alpha = [norm_next[c] / (product[c] - ratio[c] * norm_next[c] / alpha[c]) for c in each]
-        direction = [residual[c] + ratio[c] * direction[c] for c in each]
-        if iteration + 1 < CG_ITERS:
-            along = [image[c] + ratio[c] * along[c] for c in each]
-        update = [update[c] + alpha[c] * direction[c] for c in each]
-        norm_now = norm_next
+        further = None if last else apply(image)
+        for c in each:
+            if iteration == 0:
+                alpha[c] = norm_now[c] / product[c]
+                direction[c], along[c] = residual[c], image[c]
+                beyond[c] = None if last else further[c]
+                update[c] = alpha[c] * direction[c]
+            else:
+                ratio = norm_now[c] / norm_before[c]
+                alpha[c] = norm_now[c] / (product[c] - ratio * norm_now[c] / alpha[c])
+                direction[c] = residual[c] + ratio * direction[c]
+                if not last:
+                    along[c] = image[c] + ratio * along[c]
+                    beyond[c] = further[c] + ratio * beyond[c]
+                update[c] = update[c] + alpha[c] * direction[c]
+            if not last:
+                residual[c] = residual[c] - alpha[c] * along[c]
+                image[c] = image[c] - alpha[c] * beyond[c]
+        norm_before = norm_now
     return update
 
 

time: 38.4 us -> 38.2 us (level)
  no operation moved by 1% of the time
where the time goes in v2:
time: 38.2 us; the launch traced here: 38.1 us
  starting transfers between devices  18 us (47%)
  waiting for transfers between devices  13.9 us (36%)
  Pallas kernels  5.41 us (14%)
  between operations  0.75 us (2%)
    ppermute x6, starting transfers between devices, gather_tiles(): lax.ppermute(piece, 'tile', [(i, i ^ mask) for i in range(n)])  5.84 us
    ppermute x3, starting transfers between devices, exchange(): got.append(lax.ppermute(arrays[k - 1], 'survey', survey_pairs(k, n)))  5.71 us
    ppermute x3, waiting for transfers between devices, exchange(): got.append(lax.ppermute(arrays[k - 1], 'survey', survey_pairs(k, n)))  5.27 us
    ppermute x3, starting transfers between devices, exchange_across(): got.append(lax.ppermute(array, ('survey', 'tile'), pairs))  3.93 us
    ppermute x6, waiting for transfers between devices, gather_tiles(): lax.ppermute(piece, 'tile', [(i, i ^ mask) for i in range(n)])  3.84 us
    ppermute x3, waiting for transfers between devices, exchange_across(): got.append(lax.ppermute(array, ('survey', 'tile'), pairs))  2.55 us
    ppermute x8, starting transfers between devices, gather_tiles(): lax.ppermute(pieces[mask], 'tile', [(i, i ^ 1) for i in range(n)])  2.54 us
    ppermute x8, waiting for transfers between devices, gather_tiles(): lax.ppermute(pieces[mask], 'tile', [(i, i ^ 1) for i in range(n)])  2.21 us
  transfers between devices with their start and end apart: 20, of which 9 were waited for; matrix products, arithmetic and copies ran while one was open for 0% of the time, Pallas kernels for 3%

profile of v2, /device:TPU:0, one launch (start us, length us, event | category | flops | bytes accessed | tf_op | source)
XLA Modules:
  0.0 38.1 jit_solution(10465876664905349249)
XLA Ops:
  0.6 1.1 %shard_map.59 = (bf16[128,256]{1,0:T(8,128)(2,1)S(1)}, bf16[128,256]{1,0:T(8,128)(2,1)S(1)}, bf16[128,256]{1,0:T(8,128)(2,1)S(1)}, bf16[1,8,128,256]{3,2,1,0:T(8,128)(2,1)S(1)}) custom-call(s32[4,1,4,128]{3,2,1,0:T(4,128)} %index_ref.1, bf16[1,8,128,256]{3,2,1,0:T(8,128)(2,1)} %data_hbm.1), custom_call_target="tpu_custom_call" | custom-call | tf_op jit(solution)/shard_map/pallas_call | solution.py:352
  1.8 3.1 %collective-permute-start = (bf16[128,256]{1,0:T(8,128)(2,1)S(1)}, bf16[128,256]{1,0:T(8,128)(2,1)S(1)}, u32[]{:S(2)}, u32[]{:S(2)}) collective-permute-start(bf16[128,256]{1,0:T(8,128)(2,1)S(1)} %get-tuple-element.27), channel_id=1, source_target_pairs={{0,8},{8,0},{16,24},{24,16},{1,9},{9,1},{17,25},{25,17},{2,10},{10... | collective-permute-start | bytes 196616 | tf_op jit(solution)/shard_map/ppermute | solution.py:317
  4.9 2.6 %collective-permute-start.1 = (bf16[128,256]{1,0:T(8,128)(2,1)S(1)}, bf16[128,256]{1,0:T(8,128)(2,1)S(1)}, u32[]{:S(2)}, u32[]{:S(2)}) collective-permute-start(bf16[128,256]{1,0:T(8,128)(2,1)S(1)} %get-tuple-element.28), channel_id=1, source_target_pairs={{0,16},{8,24},{16,0},{24,8},{1,17},{9,25},{17,1},{25,9},{2,18},{10... | collective-permute-start | bytes 196616 | tf_op jit(solution)/shard_map/ppermute | solution.py:317
  7.5 0.8 %shard_map.60 = (bf16[512,256]{1,0:T(8,128)(2,1)S(1)}, f32[3,256,128]{2,1,0:T(8,128)S(1)}, f32[3,256,128]{2,1,0:T(8,128)S(1)}, f32[3,8,128]{2,1,0:T(8,128)S(1)},...) custom-call(s32[4,1,4,128]{3,2,1,0:T(4,128)S(1)} %copy-done, s32[4,1,4]{2,1,0:T(1,128)S(1)} %copy-done.1, ...), custom_call_target="tpu_custom_call" | custom-call | tf_op jit(solution)/shard_map/pallas_call | solution.py:360
  8.3 3.9 %collective-permute-done.1.refs_1_ = bf16[128,256]{1,0:T(8,128)(2,1)S(1)} collective-permute-done((bf16[128,256]{1,0:T(8,128)(2,1)S(1)}, bf16[128,256]{1,0:T(8,128)(2,1)S(1)}, u32[]{:S(2)}, u32[]{:S(2)}) %collective-permute-start.1) | collective-permute-done | bytes 65568 | tf_op jit(solution)/shard_map/ppermute | solution.py:317
  12.2 1.4 %collective-permute-done.2.refs_2_ = bf16[128,256]{1,0:T(8,128)(2,1)S(1)} collective-permute-done((bf16[128,256]{1,0:T(8,128)(2,1)S(1)}, bf16[128,256]{1,0:T(8,128)(2,1)S(1)}, u32[]{:S(2)}, u32[]{:S(2)}) %collective-permute-start.2) | collective-permute-done | bytes 65568 | tf_op jit(solution)/shard_map/ppermute | solution.py:317
  14.0 2.7 %collective-permute-start.6 = (f32[6,8,128]{2,1,0:T(8,128)S(1)}, f32[6,8,128]{2,1,0:T(8,128)S(1)}, u32[]{:S(2)}, u32[]{:S(2)}) collective-permute-start(f32[6,8,128]{2,1,0:T(8,128)S(1)} %shard_map.61.refs_0_), channel_id=1, source_target_pairs={{0,5},{1,4},{2,7},{3,6},{4,1},{5,0},{6,3},{7,2},{8,13},{9,12},{10,... | collective-permute-start | bytes 73736 | tf_op jit(solution)/shard_map/ppermute | solution.py:306
  16.7 0.6 %collective-permute-start.3 = (f32[6,8,128]{2,1,0:T(8,128)S(1)}, f32[6,8,128]{2,1,0:T(8,128)S(1)}, u32[]{:S(2)}, u32[]{:S(2)}) collective-permute-start(f32[6,8,128]{2,1,0:T(8,128)S(1)} %shard_map.61.refs_0_), channel_id=1, source_target_pairs={{0,1},{1,0},{2,3},{3,2},{4,5},{5,4},{6,7},{7,6},{8,9},{9,8},{10,11... | collective-permute-start | bytes 73736 | tf_op jit(solution)/shard_map/ppermute | solution.py:309
  17.6 0.7 %collective-permute-done.6.refs_5_ = f32[6,8,128]{2,1,0:T(8,128)S(1)} collective-permute-done((f32[6,8,128]{2,1,0:T(8,128)S(1)}, f32[6,8,128]{2,1,0:T(8,128)S(1)}, u32[]{:S(2)}, u32[]{:S(2)}) %collective-permute-start.6) | collective-permute-done | bytes 24608 | tf_op jit(solution)/shard_map/ppermute | solution.py:306
  18.2 0.6 %collective-permute-start.7 = (f32[6,8,128]{2,1,0:T(8,128)S(1)}, f32[6,8,128]{2,1,0:T(8,128)S(1)}, u32[]{:S(2)}, u32[]{:S(2)}) collective-permute-start(f32[6,8,128]{2,1,0:T(8,128)S(1)} %collective-permute-done.6.refs_5_), channel_id=1, source_target_pairs={{0,1},{1,0},{2,3},{3,2},{4,5},{5,4},{6,7},{7,6},{8,9},{9,8},{10,11... | collective-permute-start | bytes 73736 | tf_op jit(solution)/shard_map/ppermute | solution.py:309
  18.9 2.0 %collective-permute-done.8.refs_7_ = f32[6,8,128]{2,1,0:T(8,128)S(1)} collective-permute-done((f32[6,8,128]{2,1,0:T(8,128)S(1)}, f32[6,8,128]{2,1,0:T(8,128)S(1)}, u32[]{:S(2)}, u32[]{:S(2)}) %collective-permute-start.8) | collective-permute-done | bytes 24608 | tf_op jit(solution)/shard_map/ppermute | solution.py:306
  20.9 1.2 %collective-permute-done.9.refs_6_ = f32[6,8,128]{2,1,0:T(8,128)S(1)} collective-permute-done((f32[6,8,128]{2,1,0:T(8,128)S(1)}, f32[6,8,128]{2,1,0:T(8,128)S(1)}, u32[]{:S(2)}, u32[]{:S(2)}) %collective-permute-start.9) | collective-permute-done | bytes 24608 | tf_op jit(solution)/shard_map/ppermute | solution.py:309
  22.1 0.5 %shard_map.62 = (f32[3,8,128]{2,1,0:T(8,128)S(1)}, f32[3,8,128]{2,1,0:T(8,128)S(1)}) custom-call(f32[1,3]{1,0:T(1,128)S(1)} %bitcast.3, f32[6,8,128]{2,1,0:T(8,128)S(1)} %shard_map.61.refs_0_, f32[6,8,128]{2,1,0:T(8,128)S(1)} %collective-permute-done.3.refs_1_, f32[6,8,128]{2,1,0:T(8,128)S(1)} %collective-permute-done.5.refs_2_, ...), custom_call_target="tpu_custom_call" | custom-call | tf_op jit(solution)/shard_map/pallas_call | solution.py:369
  22.7 2.0 %collective-permute-start.11 = (f32[3,8,128]{2,1,0:T(8,128)S(1)}, f32[3,8,128]{2,1,0:T(8,128)S(1)}, u32[]{:S(2)}, u32[]{:S(2)}) collective-permute-start(f32[3,8,128]{2,1,0:T(8,128)S(1)} %get-tuple-element.37), channel_id=1, source_target_pairs={{0,17},{1,16},{2,19},{3,18},{4,21},{5,20},{6,23},{7,22},{8,25},{9,... | collective-permute-start | bytes 36872 | tf_op jit(solution)/shard_map/ppermute | solution.py:325
  24.7 1.8 %collective-permute-start.12 = (f32[3,8,128]{2,1,0:T(8,128)S(1)}, f32[3,8,128]{2,1,0:T(8,128)S(1)}, u32[]{:S(2)}, u32[]{:S(2)}) collective-permute-start(f32[3,8,128]{2,1,0:T(8,128)S(1)} %get-tuple-element.37), channel_id=1, source_target_pairs={{0,25},{1,24},{2,27},{3,26},{4,29},{5,28},{6,31},{7,30},{8,17},{9,... | collective-permute-start | bytes 36872 | tf_op jit(solution)/shard_map/ppermute | solution.py:325
  26.6 0.5 %shard_map.63 = (f32[3,256,128]{2,1,0:T(8,128)S(1)}, f32[3,256,128]{2,1,0:T(8,128)S(1)}, f32[3,8,128]{2,1,0:T(8,128)S(1)}, f32[3,256,128]{2,1,0:T(8,128)S(1)}, f32[3,256,128]{2,1,0:T(8,128)S(1)}) custom-call(f32[3,8,128]{2,1,0:T(8,128)S(1)} %get-tuple-element.30.fields_ref.before_ref, bf16[512,256]{1,0:T(8,128)(2,1)S(1)} %get-tuple-element.22.basis_ref, ...), custom_call_target="tpu_custom_call" | custom-call | tf_op jit(solution)/shard_map/pallas_call | solution.py:374
  27.1 2.5 %collective-permute-done.12.refs_2_ = f32[3,8,128]{2,1,0:T(8,128)S(1)} collective-permute-done((f32[3,8,128]{2,1,0:T(8,128)S(1)}, f32[3,8,128]{2,1,0:T(8,128)S(1)}, u32[]{:S(2)}, u32[]{:S(2)}) %collective-permute-start.12) | collective-permute-done | bytes 12320 | tf_op jit(solution)/shard_map/ppermute | solution.py:325
  30.0 0.5 %collective-permute-start.14 = (f32[6,8,128]{2,1,0:T(8,128)S(1)}, f32[6,8,128]{2,1,0:T(8,128)S(1)}, u32[]{:S(2)}, u32[]{:S(2)}) collective-permute-start(f32[6,8,128]{2,1,0:T(8,128)S(1)} %shard_map.64.refs_0_), channel_id=1, source_target_pairs={{0,3},{1,2},{2,1},{3,0},{4,7},{5,6},{6,5},{7,4},{8,11},{9,10},{10,... | collective-permute-start | bytes 73736 | tf_op jit(solution)/shard_map/ppermute | solution.py:306
  30.6 0.5 %collective-permute-start.16 = (f32[6,8,128]{2,1,0:T(8,128)S(1)}, f32[6,8,128]{2,1,0:T(8,128)S(1)}, u32[]{:S(2)}, u32[]{:S(2)}) collective-permute-start(f32[6,8,128]{2,1,0:T(8,128)S(1)} %shard_map.64.refs_0_), channel_id=1, source_target_pairs={{0,5},{1,4},{2,7},{3,6},{4,1},{5,0},{6,3},{7,2},{8,13},{9,12},{10,... | collective-permute-start | bytes 73736 | tf_op jit(solution)/shard_map/ppermute | solution.py:306
  31.0 2.1 %collective-permute-start.18 = (f32[6,8,128]{2,1,0:T(8,128)S(1)}, f32[6,8,128]{2,1,0:T(8,128)S(1)}, u32[]{:S(2)}, u32[]{:S(2)}) collective-permute-start(f32[6,8,128]{2,1,0:T(8,128)S(1)} %shard_map.64.refs_0_), channel_id=1, source_target_pairs={{0,7},{1,6},{2,5},{3,4},{4,3},{5,2},{6,1},{7,0},{8,15},{9,14},{10,... | collective-permute-start | bytes 73736 | tf_op jit(solution)/shard_map/ppermute | solution.py:306
  33.4 0.4 %collective-permute-start.15 = (f32[6,8,128]{2,1,0:T(8,128)S(1)}, f32[6,8,128]{2,1,0:T(8,128)S(1)}, u32[]{:S(2)}, u32[]{:S(2)}) collective-permute-start(f32[6,8,128]{2,1,0:T(8,128)S(1)} %collective-permute-done.14.refs_3_), channel_id=1, source_target_pairs={{0,1},{1,0},{2,3},{3,2},{4,5},{5,4},{6,7},{7,6},{8,9},{9,8},{10,11... | collective-permute-start | bytes 73736 | tf_op jit(solution)/shard_map/ppermute | solution.py:309
  34.2 1.0 %collective-permute-done.18.refs_7_ = f32[6,8,128]{2,1,0:T(8,128)S(1)} collective-permute-done((f32[6,8,128]{2,1,0:T(8,128)S(1)}, f32[6,8,128]{2,1,0:T(8,128)S(1)}, u32[]{:S(2)}, u32[]{:S(2)}) %collective-permute-start.18) | collective-permute-done | bytes 24608 | tf_op jit(solution)/shard_map/ppermute | solution.py:306
  35.3 1.0 %collective-permute-done.19.refs_6_ = f32[6,8,128]{2,1,0:T(8,128)S(1)} collective-permute-done((f32[6,8,128]{2,1,0:T(8,128)S(1)}, f32[6,8,128]{2,1,0:T(8,128)S(1)}, u32[]{:S(2)}, u32[]{:S(2)}) %collective-permute-start.19) | collective-permute-done | bytes 24608 | tf_op jit(solution)/shard_map/ppermute | solution.py:309
  36.4 1.7 %shard_map.65 = (f32[3,8,128]{2,1,0:T(8,128)}, bf16[1024,256]{1,0:T(8,128)(2,1)}) custom-call(f32[1,3]{1,0:T(1,128)S(1)} %bitcast.4, f32[3,8,128]{2,1,0:T(8,128)S(1)} %get-tuple-element.30.fields_ref.before_ref, bf16[1,8,128,256]{3,2,1,0:T(8,128)(2,1)S(1)} %get-tuple-element.21.data_ref, f32[1024,256]{1,0:T(8,128)S(1)} %get-tuple-element.31.slope_ref, ...), custom_call_target="tpu_custom_call" | custom-call | tf_op jit(solution)/shard_map/pallas_call | solution.py:383
  (29 shorter events, 2.0 us)
Async XLA Ops:
  0.6 6.9 %copy-start = (s32[4,1,4,128]{3,2,1,0:T(4,128)S(1)}, s32[4,1,4,128]{3,2,1,0:T(4,128)}, u32[]{:S(2)}) copy-start(s32[4,1,4,128]{3,2,1,0:T(4,128)} %index_ref.1) | copy-start | bytes 24580
  1.8 6.5 %collective-permute-start = (bf16[128,256]{1,0:T(8,128)(2,1)S(1)}, bf16[128,256]{1,0:T(8,128)(2,1)S(1)}, u32[]{:S(2)}, u32[]{:S(2)}) collective-permute-start(bf16[128,256]{1,0:T(8,128)(2,1)S(1)} %get-tuple-element.27), channel_id=1, source_target_pairs={{0,8},{8,0},{16,24},{24,16},{1,9},{9,1},{17,25},{25,17},{2,10},{10... | collective-permute-start | bytes 196616 | tf_op jit(solution)/shard_map/ppermute | solution.py:317
  4.9 2.6 %copy-start.1 = (s32[4,1,4]{2,1,0:T(1,128)S(1)}, s32[4,1,4]{2,1,0:T(1,128)}, u32[]{:S(2)}) copy-start(s32[4,1,4]{2,1,0:T(1,128)} %count_ref.1) | copy-start | bytes 196
  4.9 7.3 %collective-permute-start.1 = (bf16[128,256]{1,0:T(8,128)(2,1)S(1)}, bf16[128,256]{1,0:T(8,128)(2,1)S(1)}, u32[]{:S(2)}, u32[]{:S(2)}) collective-permute-start(bf16[128,256]{1,0:T(8,128)(2,1)S(1)} %get-tuple-element.28), channel_id=1, source_target_pairs={{0,16},{8,24},{16,0},{24,8},{1,17},{9,25},{17,1},{25,9},{2,18},{10... | collective-permute-start | bytes 196616 | tf_op jit(solution)/shard_map/ppermute | solution.py:317
  7.5 6.1 %collective-permute-start.2 = (bf16[128,256]{1,0:T(8,128)(2,1)S(1)}, bf16[128,256]{1,0:T(8,128)(2,1)S(1)}, u32[]{:S(2)}, u32[]{:S(2)}) collective-permute-start(bf16[128,256]{1,0:T(8,128)(2,1)S(1)} %get-tuple-element.29), channel_id=1, source_target_pairs={{0,24},{8,16},{16,8},{24,0},{1,25},{9,17},{17,9},{25,1},{2,26},{10... | collective-permute-start | bytes 196616 | tf_op jit(solution)/shard_map/ppermute | solution.py:317
  13.9 8.2 %copy-start.2 = (f32[3]{0:T(128)S(1)}, f32[3]{0:T(128)}, u32[]{:S(2)}) copy-start(f32[3]{0:T(128)} %param.7) | copy-start | bytes 40
  13.9 3.5 %collective-permute-start.4 = (f32[6,8,128]{2,1,0:T(8,128)S(1)}, f32[6,8,128]{2,1,0:T(8,128)S(1)}, u32[]{:S(2)}, u32[]{:S(2)}) collective-permute-start(f32[6,8,128]{2,1,0:T(8,128)S(1)} %shard_map.61.refs_0_), channel_id=1, source_target_pairs={{0,3},{1,2},{2,1},{3,0},{4,7},{5,6},{6,5},{7,4},{8,11},{9,10},{10,... | collective-permute-start | bytes 73736 | tf_op jit(solution)/shard_map/ppermute | solution.py:306
  14.0 4.2 %collective-permute-start.6 = (f32[6,8,128]{2,1,0:T(8,128)S(1)}, f32[6,8,128]{2,1,0:T(8,128)S(1)}, u32[]{:S(2)}, u32[]{:S(2)}) collective-permute-start(f32[6,8,128]{2,1,0:T(8,128)S(1)} %shard_map.61.refs_0_), channel_id=1, source_target_pairs={{0,5},{1,4},{2,7},{3,6},{4,1},{5,0},{6,3},{7,2},{8,13},{9,12},{10,... | collective-permute-start | bytes 73736 | tf_op jit(solution)/shard_map/ppermute | solution.py:306
  16.7 4.2 %collective-permute-start.8 = (f32[6,8,128]{2,1,0:T(8,128)S(1)}, f32[6,8,128]{2,1,0:T(8,128)S(1)}, u32[]{:S(2)}, u32[]{:S(2)}) collective-permute-start(f32[6,8,128]{2,1,0:T(8,128)S(1)} %shard_map.61.refs_0_), channel_id=1, source_target_pairs={{0,7},{1,6},{2,5},{3,4},{4,3},{5,2},{6,1},{7,0},{8,15},{9,14},{10,... | collective-permute-start | bytes 73736 | tf_op jit(solution)/shard_map/ppermute | solution.py:306
  16.7 4.1 %collective-permute-start.3 = (f32[6,8,128]{2,1,0:T(8,128)S(1)}, f32[6,8,128]{2,1,0:T(8,128)S(1)}, u32[]{:S(2)}, u32[]{:S(2)}) collective-permute-start(f32[6,8,128]{2,1,0:T(8,128)S(1)} %shard_map.61.refs_0_), channel_id=1, source_target_pairs={{0,1},{1,0},{2,3},{3,2},{4,5},{5,4},{6,7},{7,6},{8,9},{9,8},{10,11... | collective-permute-start | bytes 73736 | tf_op jit(solution)/shard_map/ppermute | solution.py:309
  17.5 3.4 %collective-permute-start.5 = (f32[6,8,128]{2,1,0:T(8,128)S(1)}, f32[6,8,128]{2,1,0:T(8,128)S(1)}, u32[]{:S(2)}, u32[]{:S(2)}) collective-permute-start(f32[6,8,128]{2,1,0:T(8,128)S(1)} %collective-permute-done.4.refs_3_), channel_id=1, source_target_pairs={{0,1},{1,0},{2,3},{3,2},{4,5},{5,4},{6,7},{7,6},{8,9},{9,8},{10,11... | collective-permute-start | bytes 73736 | tf_op jit(solution)/shard_map/ppermute | solution.py:309
  18.2 2.6 %collective-permute-start.7 = (f32[6,8,128]{2,1,0:T(8,128)S(1)}, f32[6,8,128]{2,1,0:T(8,128)S(1)}, u32[]{:S(2)}, u32[]{:S(2)}) collective-permute-start(f32[6,8,128]{2,1,0:T(8,128)S(1)} %collective-permute-done.6.refs_5_), channel_id=1, source_target_pairs={{0,1},{1,0},{2,3},{3,2},{4,5},{5,4},{6,7},{7,6},{8,9},{9,8},{10,11... | collective-permute-start | bytes 73736 | tf_op jit(solution)/shard_map/ppermute | solution.py:309
  20.9 1.2 %collective-permute-start.9 = (f32[6,8,128]{2,1,0:T(8,128)S(1)}, f32[6,8,128]{2,1,0:T(8,128)S(1)}, u32[]{:S(2)}, u32[]{:S(2)}) collective-permute-start(f32[6,8,128]{2,1,0:T(8,128)S(1)} %collective-permute-done.8.refs_7_), channel_id=1, source_target_pairs={{0,1},{1,0},{2,3},{3,2},{4,5},{5,4},{6,7},{7,6},{8,9},{9,8},{10,11... | collective-permute-start | bytes 73736 | tf_op jit(solution)/shard_map/ppermute | solution.py:309
  22.6 4.5 %collective-permute-start.10 = (f32[3,8,128]{2,1,0:T(8,128)S(1)}, f32[3,8,128]{2,1,0:T(8,128)S(1)}, u32[]{:S(2)}, u32[]{:S(2)}) collective-permute-start(f32[3,8,128]{2,1,0:T(8,128)S(1)} %get-tuple-element.37), channel_id=1, source_target_pairs={{0,9},{1,8},{2,11},{3,10},{4,13},{5,12},{6,15},{7,14},{8,1},{9,0},... | collective-permute-start | bytes 36872 | tf_op jit(solution)/shard_map/ppermute | solution.py:325
  22.7 4.4 %collective-permute-start.11 = (f32[3,8,128]{2,1,0:T(8,128)S(1)}, f32[3,8,128]{2,1,0:T(8,128)S(1)}, u32[]{:S(2)}, u32[]{:S(2)}) collective-permute-start(f32[3,8,128]{2,1,0:T(8,128)S(1)} %get-tuple-element.37), channel_id=1, source_target_pairs={{0,17},{1,16},{2,19},{3,18},{4,21},{5,20},{6,23},{7,22},{8,25},{9,... | collective-permute-start | bytes 36872 | tf_op jit(solution)/shard_map/ppermute | solution.py:325
  24.7 4.9 %collective-permute-start.12 = (f32[3,8,128]{2,1,0:T(8,128)S(1)}, f32[3,8,128]{2,1,0:T(8,128)S(1)}, u32[]{:S(2)}, u32[]{:S(2)}) collective-permute-start(f32[3,8,128]{2,1,0:T(8,128)S(1)} %get-tuple-element.37), channel_id=1, source_target_pairs={{0,25},{1,24},{2,27},{3,26},{4,29},{5,28},{6,31},{7,30},{8,17},{9,... | collective-permute-start | bytes 36872 | tf_op jit(solution)/shard_map/ppermute | solution.py:325
  30.0 3.4 %collective-permute-start.14 = (f32[6,8,128]{2,1,0:T(8,128)S(1)}, f32[6,8,128]{2,1,0:T(8,128)S(1)}, u32[]{:S(2)}, u32[]{:S(2)}) collective-permute-start(f32[6,8,128]{2,1,0:T(8,128)S(1)} %shard_map.64.refs_0_), channel_id=1, source_target_pairs={{0,3},{1,2},{2,1},{3,0},{4,7},{5,6},{6,5},{7,4},{8,11},{9,10},{10,... | collective-permute-start | bytes 73736 | tf_op jit(solution)/shard_map/ppermute | solution.py:306
  30.6 3.3 %collective-permute-start.16 = (f32[6,8,128]{2,1,0:T(8,128)S(1)}, f32[6,8,128]{2,1,0:T(8,128)S(1)}, u32[]{:S(2)}, u32[]{:S(2)}) collective-permute-start(f32[6,8,128]{2,1,0:T(8,128)S(1)} %shard_map.64.refs_0_), channel_id=1, source_target_pairs={{0,5},{1,4},{2,7},{3,6},{4,1},{5,0},{6,3},{7,2},{8,13},{9,12},{10,... | collective-permute-start | bytes 73736 | tf_op jit(solution)/shard_map/ppermute | solution.py:306
  31.0 4.2 %collective-permute-start.18 = (f32[6,8,128]{2,1,0:T(8,128)S(1)}, f32[6,8,128]{2,1,0:T(8,128)S(1)}, u32[]{:S(2)}, u32[]{:S(2)}) collective-permute-start(f32[6,8,128]{2,1,0:T(8,128)S(1)} %shard_map.64.refs_0_), channel_id=1, source_target_pairs={{0,7},{1,6},{2,5},{3,4},{4,3},{5,2},{6,1},{7,0},{8,15},{9,14},{10,... | collective-permute-start | bytes 73736 | tf_op jit(solution)/shard_map/ppermute | solution.py:306
  33.1 2.3 %collective-permute-start.13 = (f32[6,8,128]{2,1,0:T(8,128)S(1)}, f32[6,8,128]{2,1,0:T(8,128)S(1)}, u32[]{:S(2)}, u32[]{:S(2)}) collective-permute-start(f32[6,8,128]{2,1,0:T(8,128)S(1)} %shard_map.64.refs_0_), channel_id=1, source_target_pairs={{0,1},{1,0},{2,3},{3,2},{4,5},{5,4},{6,7},{7,6},{8,9},{9,8},{10,11... | collective-permute-start | bytes 73736 | tf_op jit(solution)/shard_map/ppermute | solution.py:309
  33.4 1.9 %collective-permute-start.15 = (f32[6,8,128]{2,1,0:T(8,128)S(1)}, f32[6,8,128]{2,1,0:T(8,128)S(1)}, u32[]{:S(2)}, u32[]{:S(2)}) collective-permute-start(f32[6,8,128]{2,1,0:T(8,128)S(1)} %collective-permute-done.14.refs_3_), channel_id=1, source_target_pairs={{0,1},{1,0},{2,3},{3,2},{4,5},{5,4},{6,7},{7,6},{8,9},{9,8},{10,11... | collective-permute-start | bytes 73736 | tf_op jit(solution)/shard_map/ppermute | solution.py:309
  33.8 1.5 %collective-permute-start.17 = (f32[6,8,128]{2,1,0:T(8,128)S(1)}, f32[6,8,128]{2,1,0:T(8,128)S(1)}, u32[]{:S(2)}, u32[]{:S(2)}) collective-permute-start(f32[6,8,128]{2,1,0:T(8,128)S(1)} %collective-permute-done.16.refs_5_), channel_id=1, source_target_pairs={{0,1},{1,0},{2,3},{3,2},{4,5},{5,4},{6,7},{7,6},{8,9},{9,8},{10,11... | collective-permute-start | bytes 73736 | tf_op jit(solution)/shard_map/ppermute | solution.py:309
  35.2 1.2 %collective-permute-start.19 = (f32[6,8,128]{2,1,0:T(8,128)S(1)}, f32[6,8,128]{2,1,0:T(8,128)S(1)}, u32[]{:S(2)}, u32[]{:S(2)}) collective-permute-start(f32[6,8,128]{2,1,0:T(8,128)S(1)} %collective-permute-done.18.refs_7_), channel_id=1, source_target_pairs={{0,1},{1,0},{2,3},{3,2},{4,5},{5,4},{6,7},{7,6},{8,9},{9,8},{10,11... | collective-permute-start | bytes 73736 | tf_op jit(solution)/shard_map/ppermute | solution.py:309

commit v3 on v2

--- a/solution.py
+++ b/solution.py
@@ -155,13 +155,13 @@
         sums[c] = term if sums[c] is None else sums[c] + term
 
 
-def pair_first_kernel(n, basis_ref, own_ref, moved_ref, mask_ref, energy_ref, *refs):
-    arrived, out_ref = refs[: n - 1], refs[-1]
+def pair_first_kernel(slots, basis_ref, own_ref, moved_ref, mask_ref, energy_ref, *refs):
+    arrived, before, out_ref = refs[: len(slots)], refs[len(slots) : -1], refs[-1]
     samples, rows_y = own_ref.shape[1:]
     time_pos = time_column(samples, rows_y)
-    sums = [None] * 6
-    for k in range(n - 1):
-        partner = lax.dot_general(basis_ref[:samples, :], arrived[k][...], NT, preferred_element_type=f32)
+    sums = [before[0][c] if before else None for c in range(6)]
+    for k, traces_ref in zip(slots, arrived):
+        partner = lax.dot_general(basis_ref[:samples, :], traces_ref[...], NT, preferred_element_type=f32)
         add_pair(sums, own_ref[k], moved_ref[k], partner, mask_ref[k], energy_ref, k, time_pos)
     for c in range(6):
         out_ref[c] = sums[c]
@@ -362,9 +362,14 @@
         [basis_shape, lane_shape, lane_shape, mask_shape, energy_shape, slope_shape],
         3,
     )(correlation_index, correlation_count, data)
-    terms = call(functools.partial(pair_first_kernel, n_survey), term_shape, 5 + others)(
-        basis, own, moved, mask, energy, *arrived
-    )
+    terms = []
+    for slots in (range(1, others), range(1)):
+        if len(slots):
+            terms = call(
+                functools.partial(pair_first_kernel, slots), term_shape, 5 + len(slots) + len(terms)
+            )(basis, own, moved, mask, energy, *[arrived[k] for k in slots], *terms)
+            terms = [terms]
+    terms = terms[0]
     masks, pieces = gather_tiles(terms, n_tile)
     fields, beside = call(
         functools.partial(solve_first_kernel, masks), [field_shape] * 2, 1 + n_tile, scratch_shapes=[grid]

time: 38.2 us -> 38 us (level)
  waiting for transfers between devices: 13.9 us -> 13.2 us
    ppermute x3, waiting for transfers between devices: 5.27 us -> 3.81 us  [exchange(): got.append(lax.ppermute(arrays[k - 1], 'survey', survey_pairs(k, n)))]
    ppermute x3, waiting for transfers between devices: 2.55 us -> 3.33 us  [exchange_across(): got.append(lax.ppermute(array, ('survey', 'tile'), pairs))]
  transfers between devices with their start and end apart: 20 -> 20, of which waited for: 9 -> 10; matrix products, arithmetic and copies ran while one was open for 0% -> 0% of each run, Pallas kernels for 3% -> 4%
where the time goes in v3:
time: 38 us; the launch traced here: 37.8 us
  starting transfers between devices  18.3 us (48%)
  waiting for transfers between devices  13.2 us (35%)
  Pallas kernels  5.56 us (15%)
  between operations  0.74 us (2%)
    ppermute x6, starting transfers between devices, gather_tiles(): lax.ppermute(piece, 'tile', [(i, i ^ mask) for i in range(n)])  5.85 us
    ppermute x3, starting transfers between devices, exchange(): got.append(lax.ppermute(arrays[k - 1], 'survey', survey_pairs(k, n)))  5.71 us
    ppermute x3, starting transfers between devices, exchange_across(): got.append(lax.ppermute(array, ('survey', 'tile'), pairs))  4.22 us
    ppermute x6, waiting for transfers between devices, gather_tiles(): lax.ppermute(piece, 'tile', [(i, i ^ mask) for i in range(n)])  3.85 us
    ppermute x3, waiting for transfers between devices, exchange(): got.append(lax.ppermute(arrays[k - 1], 'survey', survey_pairs(k, n)))  3.81 us
    ppermute x3, waiting for transfers between devices, exchange_across(): got.append(lax.ppermute(array, ('survey', 'tile'), pairs))  3.33 us
    ppermute x8, starting transfers between devices, gather_tiles(): lax.ppermute(pieces[mask], 'tile', [(i, i ^ 1) for i in range(n)])  2.52 us
    ppermute x8, waiting for transfers between devices, gather_tiles(): lax.ppermute(pieces[mask], 'tile', [(i, i ^ 1) for i in range(n)])  2.21 us
  transfers between devices with their start and end apart: 20, of which 10 were waited for; matrix products, arithmetic and copies ran while one was open for 0% of the time, Pallas kernels for 4%

profile of v3, /device:TPU:0, one launch (start us, length us, event | category | flops | bytes accessed | tf_op | source)
XLA Modules:
  0.0 37.8 jit_solution(10835536578060303217)
XLA Ops:
  0.6 1.1 %shard_map.59 = (bf16[128,256]{1,0:T(8,128)(2,1)S(1)}, bf16[128,256]{1,0:T(8,128)(2,1)S(1)}, bf16[128,256]{1,0:T(8,128)(2,1)S(1)}, bf16[1,8,128,256]{3,2,1,0:T(8,128)(2,1)S(1)}) custom-call(s32[4,1,4,128]{3,2,1,0:T(4,128)} %index_ref.1, bf16[1,8,128,256]{3,2,1,0:T(8,128)(2,1)} %data_hbm.1), custom_call_target="tpu_custom_call" | custom-call | tf_op jit(solution)/shard_map/pallas_call | solution.py:352
  1.8 4.1 %collective-permute-start.1 = (bf16[128,256]{1,0:T(8,128)(2,1)S(1)}, bf16[128,256]{1,0:T(8,128)(2,1)S(1)}, u32[]{:S(2)}, u32[]{:S(2)}) collective-permute-start(bf16[128,256]{1,0:T(8,128)(2,1)S(1)} %get-tuple-element.28), channel_id=1, source_target_pairs={{0,16},{8,24},{16,0},{24,8},{1,17},{9,25},{17,1},{25,9},{2,18},{10... | collective-permute-start | bytes 196616 | tf_op jit(solution)/shard_map/ppermute | solution.py:317
  5.9 1.3 %collective-permute-start.2 = (bf16[128,256]{1,0:T(8,128)(2,1)S(1)}, bf16[128,256]{1,0:T(8,128)(2,1)S(1)}, u32[]{:S(2)}, u32[]{:S(2)}) collective-permute-start(bf16[128,256]{1,0:T(8,128)(2,1)S(1)} %get-tuple-element.29), channel_id=1, source_target_pairs={{0,24},{8,16},{16,8},{24,0},{1,25},{9,17},{17,9},{25,1},{2,26},{10... | collective-permute-start | bytes 196616 | tf_op jit(solution)/shard_map/ppermute | solution.py:317
  7.5 0.8 %shard_map.60 = (bf16[512,256]{1,0:T(8,128)(2,1)S(1)}, f32[3,256,128]{2,1,0:T(8,128)S(1)}, f32[3,256,128]{2,1,0:T(8,128)S(1)}, f32[3,8,128]{2,1,0:T(8,128)S(1)},...) custom-call(s32[4,1,4,128]{3,2,1,0:T(4,128)S(1)} %copy-done, s32[4,1,4]{2,1,0:T(1,128)S(1)} %copy-done.1, ...), custom_call_target="tpu_custom_call" | custom-call | tf_op jit(solution)/shard_map/pallas_call | solution.py:360
  8.3 1.4 %collective-permute-done.1.refs_0_.refs_1_ = bf16[128,256]{1,0:T(8,128)(2,1)S(1)} collective-permute-done((bf16[128,256]{1,0:T(8,128)(2,1)S(1)}, bf16[128,256]{1,0:T(8,128)(2,1)S(1)}, u32[]{:S(2)}, u32[]{:S(2)}) %collective-permute-start.1) | collective-permute-done | bytes 65568 | tf_op jit(solution)/shard_map/ppermute | solution.py:317
  9.6 2.5 %collective-permute-done.2.refs_1_.refs_2_ = bf16[128,256]{1,0:T(8,128)(2,1)S(1)} collective-permute-done((bf16[128,256]{1,0:T(8,128)(2,1)S(1)}, bf16[128,256]{1,0:T(8,128)(2,1)S(1)}, u32[]{:S(2)}, u32[]{:S(2)}) %collective-permute-start.2) | collective-permute-done | bytes 65568 | tf_op jit(solution)/shard_map/ppermute | solution.py:317
  12.7 2.7 %collective-permute-start.6 = (f32[6,8,128]{2,1,0:T(8,128)S(1)}, f32[6,8,128]{2,1,0:T(8,128)S(1)}, u32[]{:S(2)}, u32[]{:S(2)}) collective-permute-start(f32[6,8,128]{2,1,0:T(8,128)S(1)} %shard_map.62.refs_0_), channel_id=1, source_target_pairs={{0,5},{1,4},{2,7},{3,6},{4,1},{5,0},{6,3},{7,2},{8,13},{9,12},{10,... | collective-permute-start | bytes 73736 | tf_op jit(solution)/shard_map/ppermute | solution.py:306
  15.5 0.6 %collective-permute-start.3 = (f32[6,8,128]{2,1,0:T(8,128)S(1)}, f32[6,8,128]{2,1,0:T(8,128)S(1)}, u32[]{:S(2)}, u32[]{:S(2)}) collective-permute-start(f32[6,8,128]{2,1,0:T(8,128)S(1)} %shard_map.62.refs_0_), channel_id=1, source_target_pairs={{0,1},{1,0},{2,3},{3,2},{4,5},{5,4},{6,7},{7,6},{8,9},{9,8},{10,11... | collective-permute-start | bytes 73736 | tf_op jit(solution)/shard_map/ppermute | solution.py:309
  16.3 0.7 %collective-permute-done.6.refs_5_ = f32[6,8,128]{2,1,0:T(8,128)S(1)} collective-permute-done((f32[6,8,128]{2,1,0:T(8,128)S(1)}, f32[6,8,128]{2,1,0:T(8,128)S(1)}, u32[]{:S(2)}, u32[]{:S(2)}) %collective-permute-start.6) | collective-permute-done | bytes 24608 | tf_op jit(solution)/shard_map/ppermute | solution.py:306
  17.0 0.6 %collective-permute-start.7 = (f32[6,8,128]{2,1,0:T(8,128)S(1)}, f32[6,8,128]{2,1,0:T(8,128)S(1)}, u32[]{:S(2)}, u32[]{:S(2)}) collective-permute-start(f32[6,8,128]{2,1,0:T(8,128)S(1)} %collective-permute-done.6.refs_5_), channel_id=1, source_target_pairs={{0,1},{1,0},{2,3},{3,2},{4,5},{5,4},{6,7},{7,6},{8,9},{9,8},{10,11... | collective-permute-start | bytes 73736 | tf_op jit(solution)/shard_map/ppermute | solution.py:309
  17.6 2.0 %collective-permute-done.8.refs_7_ = f32[6,8,128]{2,1,0:T(8,128)S(1)} collective-permute-done((f32[6,8,128]{2,1,0:T(8,128)S(1)}, f32[6,8,128]{2,1,0:T(8,128)S(1)}, u32[]{:S(2)}, u32[]{:S(2)}) %collective-permute-start.8) | collective-permute-done | bytes 24608 | tf_op jit(solution)/shard_map/ppermute | solution.py:306
  19.6 1.2 %collective-permute-done.9.refs_6_ = f32[6,8,128]{2,1,0:T(8,128)S(1)} collective-permute-done((f32[6,8,128]{2,1,0:T(8,128)S(1)}, f32[6,8,128]{2,1,0:T(8,128)S(1)}, u32[]{:S(2)}, u32[]{:S(2)}) %collective-permute-start.9) | collective-permute-done | bytes 24608 | tf_op jit(solution)/shard_map/ppermute | solution.py:309
  20.8 0.5 %shard_map.63 = (f32[3,8,128]{2,1,0:T(8,128)S(1)}, f32[3,8,128]{2,1,0:T(8,128)S(1)}) custom-call(f32[1,3]{1,0:T(1,128)S(1)} %bitcast.3, f32[6,8,128]{2,1,0:T(8,128)S(1)} %shard_map.62.refs_0_, f32[6,8,128]{2,1,0:T(8,128)S(1)} %collective-permute-done.3.refs_1_, f32[6,8,128]{2,1,0:T(8,128)S(1)} %collective-permute-done.5.refs_2_, ...), custom_call_target="tpu_custom_call" | custom-call | tf_op jit(solution)/shard_map/pallas_call | solution.py:374
  21.3 1.1 %collective-permute-start.10 = (f32[3,8,128]{2,1,0:T(8,128)S(1)}, f32[3,8,128]{2,1,0:T(8,128)S(1)}, u32[]{:S(2)}, u32[]{:S(2)}) collective-permute-start(f32[3,8,128]{2,1,0:T(8,128)S(1)} %get-tuple-element.37), channel_id=1, source_target_pairs={{0,9},{1,8},{2,11},{3,10},{4,13},{5,12},{6,15},{7,14},{8,1},{9,0},... | collective-permute-start | bytes 36872 | tf_op jit(solution)/shard_map/ppermute | solution.py:325
  22.4 2.1 %collective-permute-start.11 = (f32[3,8,128]{2,1,0:T(8,128)S(1)}, f32[3,8,128]{2,1,0:T(8,128)S(1)}, u32[]{:S(2)}, u32[]{:S(2)}) collective-permute-start(f32[3,8,128]{2,1,0:T(8,128)S(1)} %get-tuple-element.37), channel_id=1, source_target_pairs={{0,17},{1,16},{2,19},{3,18},{4,21},{5,20},{6,23},{7,22},{8,25},{9,... | collective-permute-start | bytes 36872 | tf_op jit(solution)/shard_map/ppermute | solution.py:325
  24.5 1.0 %collective-permute-start.12 = (f32[3,8,128]{2,1,0:T(8,128)S(1)}, f32[3,8,128]{2,1,0:T(8,128)S(1)}, u32[]{:S(2)}, u32[]{:S(2)}) collective-permute-start(f32[3,8,128]{2,1,0:T(8,128)S(1)} %get-tuple-element.37), channel_id=1, source_target_pairs={{0,25},{1,24},{2,27},{3,26},{4,29},{5,28},{6,31},{7,30},{8,17},{9,... | collective-permute-start | bytes 36872 | tf_op jit(solution)/shard_map/ppermute | solution.py:325
  25.5 0.5 %shard_map.64 = (f32[3,256,128]{2,1,0:T(8,128)S(1)}, f32[3,256,128]{2,1,0:T(8,128)S(1)}, f32[3,8,128]{2,1,0:T(8,128)S(1)}, f32[3,256,128]{2,1,0:T(8,128)S(1)}, f32[3,256,128]{2,1,0:T(8,128)S(1)}) custom-call(f32[3,8,128]{2,1,0:T(8,128)S(1)} %get-tuple-element.30.fields_ref.before_ref, bf16[512,256]{1,0:T(8,128)(2,1)S(1)} %get-tuple-element.22.basis_ref, ...), custom_call_target="tpu_custom_call" | custom-call | tf_op jit(solution)/shard_map/pallas_call | solution.py:379
  26.5 3.0 %collective-permute-done.12.refs_2_ = f32[3,8,128]{2,1,0:T(8,128)S(1)} collective-permute-done((f32[3,8,128]{2,1,0:T(8,128)S(1)}, f32[3,8,128]{2,1,0:T(8,128)S(1)}, u32[]{:S(2)}, u32[]{:S(2)}) %collective-permute-start.12) | collective-permute-done | bytes 12320 | tf_op jit(solution)/shard_map/ppermute | solution.py:325
  29.8 0.5 %collective-permute-start.14 = (f32[6,8,128]{2,1,0:T(8,128)S(1)}, f32[6,8,128]{2,1,0:T(8,128)S(1)}, u32[]{:S(2)}, u32[]{:S(2)}) collective-permute-start(f32[6,8,128]{2,1,0:T(8,128)S(1)} %shard_map.65.refs_0_), channel_id=1, source_target_pairs={{0,3},{1,2},{2,1},{3,0},{4,7},{5,6},{6,5},{7,4},{8,11},{9,10},{10,... | collective-permute-start | bytes 73736 | tf_op jit(solution)/shard_map/ppermute | solution.py:306
  30.3 0.5 %collective-permute-start.16 = (f32[6,8,128]{2,1,0:T(8,128)S(1)}, f32[6,8,128]{2,1,0:T(8,128)S(1)}, u32[]{:S(2)}, u32[]{:S(2)}) collective-permute-start(f32[6,8,128]{2,1,0:T(8,128)S(1)} %shard_map.65.refs_0_), channel_id=1, source_target_pairs={{0,5},{1,4},{2,7},{3,6},{4,1},{5,0},{6,3},{7,2},{8,13},{9,12},{10,... | collective-permute-start | bytes 73736 | tf_op jit(solution)/shard_map/ppermute | solution.py:306
  30.8 2.1 %collective-permute-start.18 = (f32[6,8,128]{2,1,0:T(8,128)S(1)}, f32[6,8,128]{2,1,0:T(8,128)S(1)}, u32[]{:S(2)}, u32[]{:S(2)}) collective-permute-start(f32[6,8,128]{2,1,0:T(8,128)S(1)} %shard_map.65.refs_0_), channel_id=1, source_target_pairs={{0,7},{1,6},{2,5},{3,4},{4,3},{5,2},{6,1},{7,0},{8,15},{9,14},{10,... | collective-permute-start | bytes 73736 | tf_op jit(solution)/shard_map/ppermute | solution.py:306
  33.9 1.0 %collective-permute-done.18.refs_7_ = f32[6,8,128]{2,1,0:T(8,128)S(1)} collective-permute-done((f32[6,8,128]{2,1,0:T(8,128)S(1)}, f32[6,8,128]{2,1,0:T(8,128)S(1)}, u32[]{:S(2)}, u32[]{:S(2)}) %collective-permute-start.18) | collective-permute-done | bytes 24608 | tf_op jit(solution)/shard_map/ppermute | solution.py:306
  35.1 1.0 %collective-permute-done.19.refs_6_ = f32[6,8,128]{2,1,0:T(8,128)S(1)} collective-permute-done((f32[6,8,128]{2,1,0:T(8,128)S(1)}, f32[6,8,128]{2,1,0:T(8,128)S(1)}, u32[]{:S(2)}, u32[]{:S(2)}) %collective-permute-start.19) | collective-permute-done | bytes 24608 | tf_op jit(solution)/shard_map/ppermute | solution.py:309
  36.1 1.7 %shard_map.66 = (f32[3,8,128]{2,1,0:T(8,128)}, bf16[1024,256]{1,0:T(8,128)(2,1)}) custom-call(f32[1,3]{1,0:T(1,128)S(1)} %bitcast.4, f32[3,8,128]{2,1,0:T(8,128)S(1)} %get-tuple-element.30.fields_ref.before_ref, bf16[1,8,128,256]{3,2,1,0:T(8,128)(2,1)S(1)} %get-tuple-element.21.data_ref, f32[1024,256]{1,0:T(8,128)S(1)} %get-tuple-element.31.slope_ref, ...), custom_call_target="tpu_custom_call" | custom-call | tf_op jit(solution)/shard_map/pallas_call | solution.py:388
  (30 shorter events, 3.1 us)
Async XLA Ops:
  0.6 6.9 %copy-start = (s32[4,1,4,128]{3,2,1,0:T(4,128)S(1)}, s32[4,1,4,128]{3,2,1,0:T(4,128)}, u32[]{:S(2)}) copy-start(s32[4,1,4,128]{3,2,1,0:T(4,128)} %index_ref.1) | copy-start | bytes 24580
  1.8 7.8 %collective-permute-start.1 = (bf16[128,256]{1,0:T(8,128)(2,1)S(1)}, bf16[128,256]{1,0:T(8,128)(2,1)S(1)}, u32[]{:S(2)}, u32[]{:S(2)}) collective-permute-start(bf16[128,256]{1,0:T(8,128)(2,1)S(1)} %get-tuple-element.28), channel_id=1, source_target_pairs={{0,16},{8,24},{16,0},{24,8},{1,17},{9,25},{17,1},{25,9},{2,18},{10... | collective-permute-start | bytes 196616 | tf_op jit(solution)/shard_map/ppermute | solution.py:317
  5.9 1.6 %copy-start.1 = (s32[4,1,4]{2,1,0:T(1,128)S(1)}, s32[4,1,4]{2,1,0:T(1,128)}, u32[]{:S(2)}) copy-start(s32[4,1,4]{2,1,0:T(1,128)} %count_ref.1) | copy-start | bytes 196
  5.9 6.2 %collective-permute-start.2 = (bf16[128,256]{1,0:T(8,128)(2,1)S(1)}, bf16[128,256]{1,0:T(8,128)(2,1)S(1)}, u32[]{:S(2)}, u32[]{:S(2)}) collective-permute-start(bf16[128,256]{1,0:T(8,128)(2,1)S(1)} %get-tuple-element.29), channel_id=1, source_target_pairs={{0,24},{8,16},{16,8},{24,0},{1,25},{9,17},{17,9},{25,1},{2,26},{10... | collective-permute-start | bytes 196616 | tf_op jit(solution)/shard_map/ppermute | solution.py:317
  7.3 5.1 %collective-permute-start = (bf16[128,256]{1,0:T(8,128)(2,1)S(1)}, bf16[128,256]{1,0:T(8,128)(2,1)S(1)}, u32[]{:S(2)}, u32[]{:S(2)}) collective-permute-start(bf16[128,256]{1,0:T(8,128)(2,1)S(1)} %get-tuple-element.27), channel_id=1, source_target_pairs={{0,8},{8,0},{16,24},{24,16},{1,9},{9,1},{17,25},{25,17},{2,10},{10... | collective-permute-start | bytes 196616 | tf_op jit(solution)/shard_map/ppermute | solution.py:317
  12.6 8.2 %copy-start.2 = (f32[3]{0:T(128)S(1)}, f32[3]{0:T(128)}, u32[]{:S(2)}) copy-start(f32[3]{0:T(128)} %param.7) | copy-start | bytes 40
  12.6 3.5 %collective-permute-start.4 = (f32[6,8,128]{2,1,0:T(8,128)S(1)}, f32[6,8,128]{2,1,0:T(8,128)S(1)}, u32[]{:S(2)}, u32[]{:S(2)}) collective-permute-start(f32[6,8,128]{2,1,0:T(8,128)S(1)} %shard_map.62.refs_0_), channel_id=1, source_target_pairs={{0,3},{1,2},{2,1},{3,0},{4,7},{5,6},{6,5},{7,4},{8,11},{9,10},{10,... | collective-permute-start | bytes 73736 | tf_op jit(solution)/shard_map/ppermute | solution.py:306
  12.7 4.2 %collective-permute-start.6 = (f32[6,8,128]{2,1,0:T(8,128)S(1)}, f32[6,8,128]{2,1,0:T(8,128)S(1)}, u32[]{:S(2)}, u32[]{:S(2)}) collective-permute-start(f32[6,8,128]{2,1,0:T(8,128)S(1)} %shard_map.62.refs_0_), channel_id=1, source_target_pairs={{0,5},{1,4},{2,7},{3,6},{4,1},{5,0},{6,3},{7,2},{8,13},{9,12},{10,... | collective-permute-start | bytes 73736 | tf_op jit(solution)/shard_map/ppermute | solution.py:306
  15.4 4.2 %collective-permute-start.8 = (f32[6,8,128]{2,1,0:T(8,128)S(1)}, f32[6,8,128]{2,1,0:T(8,128)S(1)}, u32[]{:S(2)}, u32[]{:S(2)}) collective-permute-start(f32[6,8,128]{2,1,0:T(8,128)S(1)} %shard_map.62.refs_0_), channel_id=1, source_target_pairs={{0,7},{1,6},{2,5},{3,4},{4,3},{5,2},{6,1},{7,0},{8,15},{9,14},{10,... | collective-permute-start | bytes 73736 | tf_op jit(solution)/shard_map/ppermute | solution.py:306
  15.5 4.1 %collective-permute-start.3 = (f32[6,8,128]{2,1,0:T(8,128)S(1)}, f32[6,8,128]{2,1,0:T(8,128)S(1)}, u32[]{:S(2)}, u32[]{:S(2)}) collective-permute-start(f32[6,8,128]{2,1,0:T(8,128)S(1)} %shard_map.62.refs_0_), channel_id=1, source_target_pairs={{0,1},{1,0},{2,3},{3,2},{4,5},{5,4},{6,7},{7,6},{8,9},{9,8},{10,11... | collective-permute-start | bytes 73736 | tf_op jit(solution)/shard_map/ppermute | solution.py:309
  16.2 3.4 %collective-permute-start.5 = (f32[6,8,128]{2,1,0:T(8,128)S(1)}, f32[6,8,128]{2,1,0:T(8,128)S(1)}, u32[]{:S(2)}, u32[]{:S(2)}) collective-permute-start(f32[6,8,128]{2,1,0:T(8,128)S(1)} %collective-permute-done.4.refs_3_), channel_id=1, source_target_pairs={{0,1},{1,0},{2,3},{3,2},{4,5},{5,4},{6,7},{7,6},{8,9},{9,8},{10,11... | collective-permute-start | bytes 73736 | tf_op jit(solution)/shard_map/ppermute | solution.py:309
  17.0 2.6 %collective-permute-start.7 = (f32[6,8,128]{2,1,0:T(8,128)S(1)}, f32[6,8,128]{2,1,0:T(8,128)S(1)}, u32[]{:S(2)}, u32[]{:S(2)}) collective-permute-start(f32[6,8,128]{2,1,0:T(8,128)S(1)} %collective-permute-done.6.refs_5_), channel_id=1, source_target_pairs={{0,1},{1,0},{2,3},{3,2},{4,5},{5,4},{6,7},{7,6},{8,9},{9,8},{10,11... | collective-permute-start | bytes 73736 | tf_op jit(solution)/shard_map/ppermute | solution.py:309
  19.6 1.2 %collective-permute-start.9 = (f32[6,8,128]{2,1,0:T(8,128)S(1)}, f32[6,8,128]{2,1,0:T(8,128)S(1)}, u32[]{:S(2)}, u32[]{:S(2)}) collective-permute-start(f32[6,8,128]{2,1,0:T(8,128)S(1)} %collective-permute-done.8.refs_7_), channel_id=1, source_target_pairs={{0,1},{1,0},{2,3},{3,2},{4,5},{5,4},{6,7},{7,6},{8,9},{9,8},{10,11... | collective-permute-start | bytes 73736 | tf_op jit(solution)/shard_map/ppermute | solution.py:309
  21.3 4.8 %collective-permute-start.10 = (f32[3,8,128]{2,1,0:T(8,128)S(1)}, f32[3,8,128]{2,1,0:T(8,128)S(1)}, u32[]{:S(2)}, u32[]{:S(2)}) collective-permute-start(f32[3,8,128]{2,1,0:T(8,128)S(1)} %get-tuple-element.37), channel_id=1, source_target_pairs={{0,9},{1,8},{2,11},{3,10},{4,13},{5,12},{6,15},{7,14},{8,1},{9,0},... | collective-permute-start | bytes 36872 | tf_op jit(solution)/shard_map/ppermute | solution.py:325
  22.4 4.0 %collective-permute-start.11 = (f32[3,8,128]{2,1,0:T(8,128)S(1)}, f32[3,8,128]{2,1,0:T(8,128)S(1)}, u32[]{:S(2)}, u32[]{:S(2)}) collective-permute-start(f32[3,8,128]{2,1,0:T(8,128)S(1)} %get-tuple-element.37), channel_id=1, source_target_pairs={{0,17},{1,16},{2,19},{3,18},{4,21},{5,20},{6,23},{7,22},{8,25},{9,... | collective-permute-start | bytes 36872 | tf_op jit(solution)/shard_map/ppermute | solution.py:325
  24.5 4.9 %collective-permute-start.12 = (f32[3,8,128]{2,1,0:T(8,128)S(1)}, f32[3,8,128]{2,1,0:T(8,128)S(1)}, u32[]{:S(2)}, u32[]{:S(2)}) collective-permute-start(f32[3,8,128]{2,1,0:T(8,128)S(1)} %get-tuple-element.37), channel_id=1, source_target_pairs={{0,25},{1,24},{2,27},{3,26},{4,29},{5,28},{6,31},{7,30},{8,17},{9,... | collective-permute-start | bytes 36872 | tf_op jit(solution)/shard_map/ppermute | solution.py:325
  29.8 3.4 %collective-permute-start.14 = (f32[6,8,128]{2,1,0:T(8,128)S(1)}, f32[6,8,128]{2,1,0:T(8,128)S(1)}, u32[]{:S(2)}, u32[]{:S(2)}) collective-permute-start(f32[6,8,128]{2,1,0:T(8,128)S(1)} %shard_map.65.refs_0_), channel_id=1, source_target_pairs={{0,3},{1,2},{2,1},{3,0},{4,7},{5,6},{6,5},{7,4},{8,11},{9,10},{10,... | collective-permute-start | bytes 73736 | tf_op jit(solution)/shard_map/ppermute | solution.py:306
  30.3 3.3 %collective-permute-start.16 = (f32[6,8,128]{2,1,0:T(8,128)S(1)}, f32[6,8,128]{2,1,0:T(8,128)S(1)}, u32[]{:S(2)}, u32[]{:S(2)}) collective-permute-start(f32[6,8,128]{2,1,0:T(8,128)S(1)} %shard_map.65.refs_0_), channel_id=1, source_target_pairs={{0,5},{1,4},{2,7},{3,6},{4,1},{5,0},{6,3},{7,2},{8,13},{9,12},{10,... | collective-permute-start | bytes 73736 | tf_op jit(solution)/shard_map/ppermute | solution.py:306
  30.8 4.2 %collective-permute-start.18 = (f32[6,8,128]{2,1,0:T(8,128)S(1)}, f32[6,8,128]{2,1,0:T(8,128)S(1)}, u32[]{:S(2)}, u32[]{:S(2)}) collective-permute-start(f32[6,8,128]{2,1,0:T(8,128)S(1)} %shard_map.65.refs_0_), channel_id=1, source_target_pairs={{0,7},{1,6},{2,5},{3,4},{4,3},{5,2},{6,1},{7,0},{8,15},{9,14},{10,... | collective-permute-start | bytes 73736 | tf_op jit(solution)/shard_map/ppermute | solution.py:306
  32.8 2.2 %collective-permute-start.13 = (f32[6,8,128]{2,1,0:T(8,128)S(1)}, f32[6,8,128]{2,1,0:T(8,128)S(1)}, u32[]{:S(2)}, u32[]{:S(2)}) collective-permute-start(f32[6,8,128]{2,1,0:T(8,128)S(1)} %shard_map.65.refs_0_), channel_id=1, source_target_pairs={{0,1},{1,0},{2,3},{3,2},{4,5},{5,4},{6,7},{7,6},{8,9},{9,8},{10,11... | collective-permute-start | bytes 73736 | tf_op jit(solution)/shard_map/ppermute | solution.py:309
  33.2 1.9 %collective-permute-start.15 = (f32[6,8,128]{2,1,0:T(8,128)S(1)}, f32[6,8,128]{2,1,0:T(8,128)S(1)}, u32[]{:S(2)}, u32[]{:S(2)}) collective-permute-start(f32[6,8,128]{2,1,0:T(8,128)S(1)} %collective-permute-done.14.refs_3_), channel_id=1, source_target_pairs={{0,1},{1,0},{2,3},{3,2},{4,5},{5,4},{6,7},{7,6},{8,9},{9,8},{10,11... | collective-permute-start | bytes 73736 | tf_op jit(solution)/shard_map/ppermute | solution.py:309
  33.6 1.5 %collective-permute-start.17 = (f32[6,8,128]{2,1,0:T(8,128)S(1)}, f32[6,8,128]{2,1,0:T(8,128)S(1)}, u32[]{:S(2)}, u32[]{:S(2)}) collective-permute-start(f32[6,8,128]{2,1,0:T(8,128)S(1)} %collective-permute-done.16.refs_5_), channel_id=1, source_target_pairs={{0,1},{1,0},{2,3},{3,2},{4,5},{5,4},{6,7},{7,6},{8,9},{9,8},{10,11... | collective-permute-start | bytes 73736 | tf_op jit(solution)/shard_map/ppermute | solution.py:309
  34.9 1.2 %collective-permute-start.19 = (f32[6,8,128]{2,1,0:T(8,128)S(1)}, f32[6,8,128]{2,1,0:T(8,128)S(1)}, u32[]{:S(2)}, u32[]{:S(2)}) collective-permute-start(f32[6,8,128]{2,1,0:T(8,128)S(1)} %collective-permute-done.18.refs_7_), channel_id=1, source_target_pairs={{0,1},{1,0},{2,3},{3,2},{4,5},{5,4},{6,7},{7,6},{8,9},{9,8},{10,11... | collective-permute-start | bytes 73736 | tf_op jit(solution)/shard_map/ppermute | solution.py:309
